TPU v7x, 256 devices: a whole 4x4x8 slice. The times are simulated.
256 devices in a mesh: dp: 4 (over y), center: 64 (over x, z, core).
Axes of the slice: x: 4, y: 4, z: 8, core: 2. Of those that a mesh axis runs over, the one named last changes fastest.
Arguments:
- embeddings: bfloat16 [8192, 512], P(('dp', 'center')), may hold values from -0.59765625 to 0.59765625
- labels: int32 [8192], P(('dp', 'center')), may hold values from 0 to 10002431, as said below
- centers: bfloat16 [768, 128, 512], P('center'), may hold values from -0.25 to 0.25
- momentum: float32 [768, 128, 512], P('center'), may hold values from -6 to 6
- block_list: int32 [768], P('center'), may hold values from -1 to 78143, as said below
- counts: int32 [64], P('center'), may hold values from 4 to 12, as said below
Outputs:
- loss: float32 [8192], P(('dp', 'center'))
- embed_grad: float32 [8192, 512], P(('dp', 'center'))
- new_centers: bfloat16 [768, 128, 512], P('center')
- new_momentum: float32 [768, 128, 512], P('center')
Inputs may be any that keep to these rules, and one draw needn't show every extreme that they name: Center device j has 12 slots; its first counts[j] slots are live and some device has all 12 live. `block_list`: live slot s of center device j holds a block id of j * 1221 to (j + 1) * 1221 - 1, all live ids distinct; every other slot holds -1. The block labels[b] // 128 of every label is held in a live slot.
All inputs are finite; a program needn't handle non-finite values.
Results may differ from a plain program's by a relative error of at most 0.009.
Values may be sent and summed in bfloat16 or wider, within the bound.
A program may use at most 192 MiB of HBM per device.

v0:
```python
import math

import jax
import jax.numpy as jnp
from jax import lax
from jax.sharding import PartitionSpec as P

logit_scale = 64.0
margin_cos = 0.35
momentum_rate = 0.9
learn_rate = 0.1
tiny_eps = 1e-06


def unit_rows(values):
    squares = jnp.sum(values * values, axis=-1, keepdims=True)
    norms = jnp.sqrt(squares + tiny_eps)
    return (values / norms, norms)


def update_tiles(grad_unit, w_shard, w_unit, w_norm, v_shard, live_tile):
    grad_w = (grad_unit - w_unit * jnp.sum(w_unit * grad_unit, axis=-1, keepdims=True)) / w_norm
    new_v = jnp.where(live_tile, momentum_rate * v_shard + grad_w, v_shard)
    new_w = jnp.where(
        live_tile, (w_shard.astype(jnp.float32) - learn_rate * new_v).astype(jnp.bfloat16), w_shard
    )
    return (new_w, new_v)


def on_device(embeddings, labels, centers, momentum, block_list, counts):
    rows_dev = embeddings.shape[0]
    slots, blk_size, width = centers.shape
    flat = slots * blk_size
    x_float = embeddings.astype(jnp.float32)
    x_unit, x_norm = unit_rows(x_float)
    x_bf = x_unit.astype(jnp.bfloat16)
    group_x, group_labels = (
        lax.all_gather(x_bf, "center", axis=0, tiled=True),
        lax.all_gather(labels, "center", axis=0, tiled=True),
    )
    group_count = group_x.shape[0]
    w_float = centers.astype(jnp.float32)
    w_unit, w_norm = unit_rows(w_float)
    w_bf = w_unit.astype(jnp.bfloat16).reshape(flat, width)
    slot_iota = jnp.arange(slots, dtype=jnp.int32)
    live_slot = slot_iota < counts[0]
    live_cols = jnp.broadcast_to(live_slot[:, None], (slots, blk_size)).reshape(flat)
    col_iota = jnp.arange(blk_size, dtype=jnp.int32)
    label_block = group_labels // blk_size
    label_col = group_labels % blk_size
    hit_mask = (block_list[None, :, None] == label_block[:, None, None]) & (
        col_iota[None, None, :] == label_col[:, None, None]
    )
    hit_float = hit_mask.astype(jnp.float32).reshape(group_count, flat)
    step_rows = math.gcd(group_count, 512)
    block_total = group_count // step_rows

    def first_pass(inputs):
        x_block, hit_block = inputs
        cosine = lax.dot_general(
            x_block, w_bf, (((1,), (1,)), ((), ())), preferred_element_type=jnp.float32
        )
        logit = logit_scale * cosine - logit_scale * margin_cos * hit_block
        exp_z = jnp.where(live_cols[None, :], jnp.exp(logit), 0.0)
        return (exp_z, jnp.sum(exp_z, axis=1), jnp.sum(hit_block * logit, axis=1))

    exp_z, part_total, part_pos = lax.map(
        first_pass,
        (
            group_x.reshape(block_total, step_rows, width),
            hit_float.reshape(block_total, step_rows, flat),
        ),
    )
    exp_z = exp_z.reshape(group_count, flat)
    total, pos_logit = lax.psum(
        (part_total.reshape(group_count), part_pos.reshape(group_count)), "center"
    )
    my_start = lax.axis_index("center") * rows_dev
    loss = lax.dynamic_slice_in_dim(jnp.log(total) - pos_logit, my_start, rows_dev, 0)
    err_bf = (logit_scale * (exp_z / total[:, None] - hit_float)).astype(jnp.bfloat16)
    grad_all = lax.psum(jnp.dot(err_bf, w_bf, preferred_element_type=jnp.float32), "center")
    grad_x = lax.dynamic_slice_in_dim(grad_all, my_start, rows_dev, 0)
    embed_grad = (grad_x - x_unit * jnp.sum(x_unit * grad_x, axis=-1, keepdims=True)) / x_norm
    grad_unit = lax.dot_general(
        err_bf, group_x, (((0,), (0,)), ((), ())), preferred_element_type=jnp.float32
    ).reshape(slots, blk_size, width)
    live_tile = live_slot[:, None, None]
    grad_sum = lax.psum(grad_unit.astype(jnp.bfloat16), "dp").astype(jnp.float32)
    new_w, new_v = update_tiles(grad_sum, centers, w_unit, w_norm, momentum, live_tile)
    return (loss, embed_grad, new_w, new_v)


def solution(mesh):
    return jax.shard_map(
        on_device,
        mesh=mesh,
        in_specs=(
            P(("dp", "center"), None),
            P(("dp", "center")),
            P("center", None, None),
            P("center", None, None),
            P("center"),
            P("center"),
        ),
        out_specs=(
            P(("dp", "center")),
            P(("dp", "center"), None),
            P("center", None, None),
            P("center", None, None),
        ),
        check_vma=False,
    )
```

profile of v0, /device:TPU:1, one launch (start us, length us, event | category | flops | bytes accessed | tf_op | source)
XLA Modules:
  0.0 721.5 jit_solution(709776395275041188)
XLA Ops:
  8.1 1.5 fusion.27
  10.3 1.3 dynamic-slice
  13.1 21.1 %all-reduce = s32[2048]{0:T(1024)S(1)} all-reduce(s32[2048]{0:T(1024)S(1)} %dynamic-update-slice), channel_id=1, replica_groups=mesh['dp'=4,'center'=64] {'center'}, use_global_device_ids=true, to_apply=%add | all-reduce | flops 2048 | bytes 16384
  35.1 6.1 and_convert_fusion
  41.3 15.7 %reshape.126 = f32[4,512,1536]{1,0,2:T(4,128)} reshape(f32[2048,12,128]{0,2,1:T(8,128)} %and_convert_fusion) | data formatting | bytes 25165824 | tf_op jit(solution)/shard_map/convert_element_type | solution.py:54
  57.4 1.5 fusion.23
  58.9 33.9 %all-gather.2.cloned.1.call-done = bf16[2048,512]{1,0:T(8,128)(2,1)} async-done(((bf16[32,512]{1,0:T(8,128)(2,1)}), bf16[2048,512]{1,0:T(8,128)(2,1)}) %all-gather.2.cloned.1.call-update) | async-done | bytes 2097168 | tf_op jit(solution)/shard_map/all_gather | solution.py:38
  92.8 82.5 %while.15 = (s32[]{:T(128)}, f32[4,512,1536]{2,1,0:T(8,128)}, f32[4,512]{1,0:T(4,128)S(1)}, f32[4,512]{1,0:T(4,128)S(1)}, bf16[4,512,512]{2,1,0:T(8,128)(2,1)}, ...) while((s32[]{:T(128)}, f32[4,512,1536]{2,1,0:T(8,128)}, ...), condition=%wide.region_5.6_spmd.clone, body=%wide.region_2.5_spmd.clone.sunk | while | flops 811596800 | bytes 30426756 | solution.py:67
  92.9 8.4 %constant_dynamic-slice_fusion.2 = f32[1,512,1536]{1,0,2:T(1,128)} fusion(f32[4,512,1536]{1,0,2:T(4,128)} %get-tuple-element.187, s32[]{:T(128)S(6)} %copy.29), kind=kLoop, calls=%fused_computation.12.clone.1 | loop fusion | bytes 6291460 | tf_op jit(solution)/shard_map/while/body/jit(dynamic_index_in_dim)/dynamic_slice | solution.py:67
  101.3 6.8 copy.20
  108.1 4.4 bitcast_dynamic-update-slice_fusion.2
  113.5 8.4 %constant_dynamic-slice_fusion.2 = f32[1,512,1536]{1,0,2:T(1,128)} fusion(f32[4,512,1536]{1,0,2:T(4,128)} %get-tuple-element.187, s32[]{:T(128)S(6)} %copy.29), kind=kLoop, calls=%fused_computation.12.clone.1 | loop fusion | bytes 6291460 | tf_op jit(solution)/shard_map/while/body/jit(dynamic_index_in_dim)/dynamic_slice | solution.py:67
  121.9 6.8 copy.20
  128.7 4.5 bitcast_dynamic-update-slice_fusion.2
  134.1 8.4 %constant_dynamic-slice_fusion.2 = f32[1,512,1536]{1,0,2:T(1,128)} fusion(f32[4,512,1536]{1,0,2:T(4,128)} %get-tuple-element.187, s32[]{:T(128)S(6)} %copy.29), kind=kLoop, calls=%fused_computation.12.clone.1 | loop fusion | bytes 6291460 | tf_op jit(solution)/shard_map/while/body/jit(dynamic_index_in_dim)/dynamic_slice | solution.py:67
  142.6 6.8 copy.20
  149.3 4.5 bitcast_dynamic-update-slice_fusion.2
  154.8 8.4 %constant_dynamic-slice_fusion.2 = f32[1,512,1536]{1,0,2:T(1,128)} fusion(f32[4,512,1536]{1,0,2:T(4,128)} %get-tuple-element.187, s32[]{:T(128)S(6)} %copy.29), kind=kLoop, calls=%fused_computation.12.clone.1 | loop fusion | bytes 6291460 | tf_op jit(solution)/shard_map/while/body/jit(dynamic_index_in_dim)/dynamic_slice | solution.py:67
  163.2 6.8 copy.20
  170.0 4.4 bitcast_dynamic-update-slice_fusion.2
  175.3 243.3 %all-reduce.1 = (f32[2048]{0:T(1024)S(1)}, f32[2048]{0:T(1024)S(1)}) all-reduce(f32[2048]{0:T(1024)S(1)} %bitcast.75, f32[2048]{0:T(1024)S(1)} %bitcast.76), channel_id=1, replica_groups=mesh['dp'=4,'center'=64] {'center'}, use_global_device_ids=true, to_apply=%region_7.8 | all-reduce | flops 4096 | bytes 32768 | tf_op jit(solution)/shard_map/psum | solution.py:75
  418.6 15.1 %copy.12 = f32[4,512,1536]{1,0,2:T(4,128)} copy(f32[4,512,1536]{2,1,0:T(8,128)} %get-tuple-element.50) | data formatting | bytes 25165824 | tf_op jit(solution)/shard_map/while | solution.py:67
  433.7 12.6 %copy.14 = f32[2048,1536]{0,1:T(8,128)} copy(f32[2048,1536]{1,0:T(8,128)} %bitcast.67) | data formatting | bytes 25165824 | tf_op jit(solution)/shard_map/reshape | solution.py:74
  446.3 9.7 %fusion.10 = bf16[2048,1536]{0,1:T(8,128)(2,1)S(1)} fusion(f32[2048,12,128]{0,2,1:T(8,128)} %and_convert_fusion, f32[2048,1536]{0,1:T(8,128)} %copy.14, f32[2048]{0:T(1024)S(1)} %get-tuple-element.97), kind=kLoop, calls=%fused_computation.18 | loop fusion | flops 12582912 | bytes 31465472 | tf_op jit(solution)/shard_map/convert_element_type | solution.py:80
  455.9 4.5 fusion.20
  460.7 10.3 %multiply_convert_fusion = bf16[4,512,1536]{1,0,2:T(4,128)(2,1)S(1)} fusion(f32[4,512,1536]{1,0,2:T(4,128)} %get-tuple-element.194, f32[4,512,1536]{1,0,2:T(4,128)} %copy.12, f32[4,512]{1,0:T(4,128)S(1)} %div.63), kind=kLoop, calls=%fused_computation.19 | loop fusion | flops 12582912 | bytes 31465472 | tf_op jit(solution)/shard_map/convert_element_type | solution.py:80
  471.0 2.7 copy.18
  473.7 5.0 fusion.28
  479.4 35.4 %all-reduce.7.cloned.1.call-done = bf16[12,128,512]{2,1,0:T(8,128)(2,1)} async-done(((bf16[12,128,512]{2,1,0:T(8,128)(2,1)}), bf16[12,128,512]{2,1,0:T(8,128)(2,1)}) %all-reduce.7.cloned.1.call-update) | async-done | bytes 1572880 | tf_op jit(solution)/shard_map/psum | solution.py:88
  514.8 13.6 %fusion.16 = (bf16[12,128,512]{2,1,0:T(8,128)(2,1)}, f32[12,128,512]{2,1,0:T(8,128)}) fusion(bf16[12,128,512]{2,1,0:T(8,128)(2,1)S(1)} %copy-done.2, pred[12]{0:T(512)(128)(4,1)S(1)} %get-tuple-element.204, f32[12,128,512]{2,1,0:T(8,128)} %param.11, bf16[12,128,512]{2,1,0:T(8,128)(2,1)} %all-reduce.7.cloned.1.call-done, f32[12,128]{1,0:T(8,128)S(1)} %add_sqrt_fusion), kind=kOutput, calls=%fused_computation.31 | output fusion | flops 13371391 | bytes 11016204 | tf_op jit(solution)/shard_map/mul | solution.py:22
  528.4 184.0 %all-reduce.5.cloned.1.call-done = f32[2048,512]{1,0:T(8,128)} async-done(((f32[2048,512]{1,0:T(8,128)}), f32[2048,512]{1,0:T(8,128)}) %all-reduce.5.cloned.1.call-update) | async-done | bytes 4194320 | tf_op jit(solution)/shard_map/psum | solution.py:81
  713.4 1.6 subtract_divide_fusion
  (50 shorter events, 8.6 us)
Async XLA Ops:
  7.2 85.6 %all-gather.2.cloned.1.call-start = ((), (), s32[]{:S(2)}) async-start(), calls=%async_computation | async-start | bytes 2129920 | tf_op jit(solution)/shard_map/all_gather | solution.py:38
  9.6 505.2 %all-reduce.7.cloned.1.call-start = ((), (), s32[]{:S(2)}) async-start(), calls=%async_computation.2 | async-start | bytes 3145728 | tf_op jit(solution)/shard_map/psum | solution.py:88
  41.3 15.7 %copy-start.1 = (bf16[12,128,512]{2,1,0:T(8,128)(2,1)S(1)}, bf16[12,128,512]{2,1,0:T(8,128)(2,1)}, u32[]{:S(2)}) copy-start(bf16[12,128,512]{2,1,0:T(8,128)(2,1)} %param.10) | copy-start | bytes 4718596
  446.3 9.7 %copy-start.3 = (bf16[4,512,512]{2,1,0:T(8,128)(2,1)S(1)}, bf16[4,512,512]{2,1,0:T(8,128)(2,1)}, u32[]{:S(2)}) copy-start(bf16[4,512,512]{2,1,0:T(8,128)(2,1)} %get-tuple-element.199) | copy-start | bytes 6291460
  460.5 251.9 %all-reduce.5.cloned.1.call-start = ((), (), s32[]{:S(2)}) async-start(), calls=%async_computation.1 | async-start | bytes 8388608 | tf_op jit(solution)/shard_map/psum | solution.py:81
  471.0 2.7 copy-start
  478.8 36.0 %copy-start.2 = (bf16[12,128,512]{2,1,0:T(8,128)(2,1)S(1)}, bf16[12,128,512]{2,1,0:T(8,128)(2,1)}, u32[]{:S(2)}) copy-start(bf16[12,128,512]{2,1,0:T(8,128)(2,1)} %param.10) | copy-start | bytes 4718596
  479.4 233.0 %copy-start.4 = (bf16[32,512]{1,0:T(8,128)(2,1)S(1)}, bf16[32,512]{1,0:T(8,128)(2,1)}, u32[]{:S(2)}) copy-start(bf16[32,512]{1,0:T(8,128)(2,1)} %param.8) | copy-start | bytes 98308
Sparse Core Ops, SparseCore 0:
  11.3 81.4 all-gather.1
  460.6 54.1 all-reduce.6
  518.3 194.0 all-reduce.4
where the time goes:
time: 724 us; the launch traced here: 721 us
  blocking collectives  264 us (36%)
  waiting for transfers between devices  253 us (35%)
  local copies, waits for them, and re-layouts  110 us (15%)
  other arithmetic  51 us (7%)
  matrix products  27.4 us (4%)
  between operations  15.2 us (2%)
    psum x1, blocking collectives, on_device(): lax.psum((part_total.reshape(group_count), part_pos.reshape(group_count))...  243 us
    psum x1, waiting for transfers between devices, on_device(): lax.psum(jnp.dot(err_bf, w_bf, preferred_element_type=jnp.float32), 'cent...  184 us
    dynamic_slice x8, local copies, waits for them, and re-layouts, on_device(): lax.map(first_pass, (group_x.reshape(block_total, step_rows, width), hit_...  60.9 us
    psum x1, waiting for transfers between devices, on_device(): lax.psum(grad_unit.astype(jnp.bfloat16), 'dp').astype(jnp.float32)  35.4 us
    all_gather x1, waiting for transfers between devices, on_device(): lax.all_gather(x_bf, 'center', axis=0, tiled=True)  33.9 us
    unnamed x1, blocking collectives  21.1 us
    convert_element_type x2, other arithmetic, on_device(): (logit_scale * (exp_z / total[:, None] - hit_float)).astype(jnp.bfloat16)  20 us
    dot_general x4, matrix products, first_pass(): lax.dot_general(x_block, w_bf, (((1,), (1,)), ((), ())), preferred_elemen...  17.9 us
  transfers between devices with their start and end apart: 3, of which 3 were waited for; matrix products, arithmetic and copies ran while one was open for 8% of the time, Pallas kernels for 0%

commit v1 on v0

v1 whole, which is shorter than its diff:
```python
import math

import jax
import jax.numpy as jnp
from jax import lax
from jax.experimental import pallas as pl
from jax.experimental.pallas import tpu as pltpu
from jax.sharding import PartitionSpec as P

MESH = pl.DeviceIdType.MESH
NX, NZ, NC, NY = 4, 8, 2, 4
f32, bf16, i32 = jnp.float32, jnp.bfloat16, jnp.int32

scale = 64.0
margin = 0.35
momentum_rate = 0.9
learn_rate = 0.1
tiny_eps = 1e-06
log2e = math.log2(math.e)
dead_bias = -1e30


def nt_dot(a, b):
    return lax.dot_general(a, b, (((1,), (1,)), ((), ())), preferred_element_type=f32)


def nn_dot(a, b):
    return lax.dot_general(a, b, (((1,), (0,)), ((), ())), preferred_element_type=f32)


def kernel(
    emb_ref, lab_ref, ids_ref, cnt_ref, cen_hbm, mom_hbm,
    loss_ref, eg_ref, nw_hbm, nv_hbm,
    cen, mom, wbf, wT, wn, xg, labs, labz, tgt, ez, err, tp, pp, t1, t2, p1, p2, inv,
    pt, pown, gs, rA2, rB2, rP, rM,
    gown, goth, pr, xs, xr, zs, zr,
    ldsem, stsem,
    xa_s, xa_r, la_s, la_r, lz_s, lz_r, zr_s, zr_r, sb_s, sb_r,
    t1_s, t1_r, t2_s, t2_r, p1_s, p1_r, p2_s, p2_r,
    ys_s, ys_r, yg_s, yg_r, pr_s, pr_r, xs_s, xs_r, zs_s, zs_r,
):
    rows = emb_ref.shape[0]
    width = emb_ref.shape[1]
    cols = cen.shape[0]
    quart = cols // NY
    half = quart // 2
    slots = cols // 128
    zrows = NC * NX * rows
    yy = lax.axis_index("dp")
    ce = lax.axis_index("center")
    xx = ce // (NZ * NC)
    zz = (ce // NC) % NZ
    cc = ce % NC

    def dev(y, x, z, c):
        return (y % NY, ((x % NX) * NZ + z % NZ) * NC + c)

    def copy(src, dst, ssem, rsem, to):
        return pltpu.make_async_remote_copy(
            src_ref=src, dst_ref=dst, send_sem=ssem, recv_sem=rsem, device_id=to, device_id_type=MESH
        )

    me = (yy, ce)
    sib = dev(yy, xx, zz, 1 - cc)

    def landed(dst, rsem):
        copy(dst, dst, rsem, rsem, sib).wait_recv()

    xc_peers = [(dx, dc) for dx in range(NX) for dc in range(NC) if (dx, dc) != (0, 0)]
    sends = []

    def send(src, dst, ssem, rsem, to):
        c = copy(src, dst, ssem, rsem, to)
        c.start()
        sends.append(c)

    ld_cen = pltpu.make_async_copy(cen_hbm, cen, ldsem.at[0])
    ld_mom = pltpu.make_async_copy(mom_hbm, mom, ldsem.at[1])
    ld_cen.start()
    ld_mom.start()
    barrier = pltpu.get_barrier_semaphore()
    greet = [dev(yy, xx + dx, zz, (cc + dc) % NC) for dx, dc in xc_peers]
    greet += [dev(yy, xx, zz + dz, cc) for dz in range(1, NZ)]
    greet += [dev(yy + 1, xx, zz, cc), dev(yy + NY - 1, xx, zz, cc)]
    for d in greet:
        pl.semaphore_signal(barrier, inc=1, device_id=d, device_id_type=MESH)

    xf = emb_ref[...].astype(f32)
    xn = jnp.sqrt(jnp.sum(xf * xf, axis=1, keepdims=True) + tiny_eps)
    xu = xf / xn
    xrow = pl.multiple_of(xx * rows, rows)
    xg[zz, cc, pl.ds(xrow, rows), :] = xu.astype(bf16)
    lab = lab_ref[...]
    lane = lax.broadcasted_iota(i32, (1, 128), 1)
    labs[0] = jnp.where(lane // rows == xx, lab, 0)
    pl.semaphore_wait(barrier, len(greet))

    for k in range(1, NX):
        blk = xg.at[zz, cc, pl.ds(xrow, rows), :]
        send(blk, blk, xa_s.at[k - 1], xa_r.at[k - 1], dev(yy, xx + k, zz, cc))
    for k, (dx, dc) in enumerate(xc_peers):
        send(labs.at[0], labs.at[dx * NC + dc], la_s.at[k], la_r.at[k], dev(yy, xx + dx, zz, (cc + dc) % NC))

    ld_cen.wait()

    @pl.loop(0, slots)
    def _(s):
        r = pl.ds(pl.multiple_of(s * 128, 128), 128)
        wf = cen[r, :].astype(f32)
        n = jnp.sqrt(jnp.sum(wf * wf, axis=1, keepdims=True) + tiny_eps)
        wn[r, :] = n
        wbf[r, :] = (wf * (1.0 / n)).astype(bf16)

    for k in range(1, NX):
        blk = xg.at[zz, cc, pl.ds(pl.multiple_of(((xx + NX - k) % NX) * rows, rows), rows), :]
        landed(blk, xa_r.at[k - 1])
    up, down = dev(yy, xx, zz + 1, cc), dev(yy, xx, zz + NZ - 1, cc)

    def piece(dz):
        return xg.at[(zz + dz + NZ) % NZ, cc]

    def halfpiece(dz, h):
        return xg.at[(zz + dz + NZ) % NZ, cc, pl.ds(h * 64, 64), :]

    def sib_half(dz, h, c):
        return xg.at[(zz + dz + NZ) % NZ, c, pl.ds(h * 64, 64), :]

    send(piece(0), piece(0), zr_s.at[0, 0], zr_r.at[0, 0], up)
    send(piece(0), piece(0), zr_s.at[1, 0], zr_r.at[1, 0], down)
    send(piece(0), piece(0), sb_s.at[0], sb_r.at[0], sib)

    for k, (dx, dc) in enumerate(xc_peers):
        landed(labs.at[dx * NC + dc], la_r.at[k])
    same, other = labs[0], labs[1]
    for dx in range(1, NX):
        same = same + labs[dx * NC]
        other = other + labs[dx * NC + 1]
    labz[zz, 0] = jnp.where(cc == 0, same, other)
    labz[zz, 1] = jnp.where(cc == 0, other, same)
    for dz in range(1, NZ):
        send(labz.at[zz], labz.at[zz], lz_s.at[dz - 1], lz_r.at[dz - 1], dev(yy, xx, zz + dz, cc))
    for dz in range(1, NZ):
        landed(labz.at[(zz + NZ - dz) % NZ], lz_r.at[dz - 1])
    for z in range(NZ):
        lb = jnp.concatenate([labz[z, 0], labz[z, 1]], axis=1)
        blk_id = lb // 128
        t = jnp.full(lb.shape, -1, i32)
        for s in range(slots):
            t = jnp.where(blk_id == ids_ref[s], s * 128 + lb % 128, t)
        tgt[z] = t

    live_count = cnt_ref[0]
    k2 = scale * log2e
    hit_bias = -scale * margin * log2e
    group = 4 if slots % 4 == 0 else 1

    def first_pass(dz):
        z = (zz + dz + NZ) % NZ
        xc = xg[z].reshape(zrows, width)
        tz = tgt[z]
        iota = lax.broadcasted_iota(i32, (128, zrows), 0)
        lanes = pl.ds(pl.multiple_of(z * zrows, zrows), zrows)

        def body(g, carry):
            tot, pos = carry
            r0 = pl.multiple_of(g * (group * 128), 128)
            s = nt_dot(wbf[pl.ds(r0, group * 128), :], xc)
            for u in range(group):
                slot = g * group + u
                su = s[u * 128:(u + 1) * 128]
                hit = iota == (tz - slot * 128)
                bias = jnp.where(slot < live_count, 0.0, dead_bias)
                e = jnp.exp2(su * k2 + jnp.where(hit, hit_bias, bias))
                ez[pl.ds(r0 + u * 128, 128), lanes] = e
                tot = tot + jnp.sum(e, axis=0, keepdims=True)
                pos = pos + jnp.sum(jnp.where(hit, su, 0.0), axis=0, keepdims=True)
            return tot, pos

        zero = jnp.zeros((1, zrows), f32)
        tot, pos = lax.fori_loop(0, slots // group, body, (zero, zero))
        tp[pl.ds(z, 1), :] = tot
        pp[pl.ds(z, 1), :] = pos

    def sib_piece(dz):
        return xg.at[(zz + dz + NZ) % NZ, 1 - cc]

    landed(sib_piece(0), sb_r.at[0])
    first_pass(0)
    for hop in range(1, NZ // 2):
        for way, to, sign in ((0, up, -1), (1, down, 1)):
            p = piece(sign * hop)
            landed(p, zr_r.at[way, hop - 1])
            if hop < NZ // 2 - 1:
                send(p, p, zr_s.at[way, hop], zr_r.at[way, hop], to)
            else:
                hp = halfpiece(sign * hop, way)
                send(hp, hp, zr_s.at[way, hop], zr_r.at[way, hop], to)
            k = 2 * hop - 1 + way
            send(p, p, sb_s.at[k], sb_r.at[k], sib)
        for way, sign in ((0, -1), (1, 1)):
            landed(sib_piece(sign * hop), sb_r.at[2 * hop - 1 + way])
            first_pass(sign * hop)
    far = NZ // 2
    for way, sign in ((0, -1), (1, 1)):
        hp = halfpiece(sign * far, way)
        landed(hp, zr_r.at[way, far - 1])
        k = 2 * far - 1 + way
        send(hp, hp, sb_s.at[k], sb_r.at[k], sib)

    @pl.loop(0, slots)
    def _(s):
        c0 = pl.multiple_of(s * 128, 128)
        wT[:, pl.ds(c0, 128)] = wbf[pl.ds(c0, 128), :].T

    for way, sign in ((0, -1), (1, 1)):
        landed(sib_half(sign * far, way, 1 - cc), sb_r.at[2 * far - 1 + way])
    first_pass(far)

    def reduce_plane(part, first, second, s1, r1, s2, r2):
        for k, (dx, dc) in enumerate(xc_peers):
            send(part, first.at[k], s1.at[k], r1.at[k], dev(yy, xx + dx, zz, (cc + dc) % NC))

        def middle():
            acc = part[...]
            for k in range(len(xc_peers)):
                landed(first.at[k], r1.at[k])
                acc = acc + first[k]
            second[0] = acc
            for dz in range(1, NZ):
                send(second.at[0], second.at[dz], s2.at[dz - 1], r2.at[dz - 1], dev(yy, xx, zz + dz, cc))

        def last():
            acc = second[0]
            for dz in range(1, NZ):
                landed(second.at[dz], r2.at[dz - 1])
                acc = acc + second[dz]
            return acc

        return middle, last

    tot_mid, tot_last = reduce_plane(tp, t1, t2, t1_s, t1_r, t2_s, t2_r)
    pos_mid, pos_last = reduce_plane(pp, p1, p2, p1_s, p1_r, p2_s, p2_r)
    tot_mid()
    pos_mid()
    total = tot_last()
    inv[...] = scale / total

    def errors(q):
        @pl.loop(0, NZ)
        def _(z):
            lanes = pl.ds(pl.multiple_of(z * zrows, zrows), zrows)
            iota = lax.broadcasted_iota(i32, (128, zrows), 0)
            iz = inv[pl.ds(z, 1), :]
            tz = tgt[z]
            for u in range(quart // 128):
                r0 = pl.multiple_of(q * quart + u * 128, 128)
                hit = iota == (tz - r0)
                e = ez[pl.ds(r0, 128), lanes] * iz - jnp.where(hit, scale, 0.0)
                err[pl.ds(r0, 128), lanes] = e.astype(bf16)

    def center_grad(q):
        r0 = pl.multiple_of(q * quart, 128)
        return nn_dot(err[pl.ds(r0, quart), :], xg[...].reshape(NZ * zrows, width))

    yup, ydn = dev(yy + 1, xx, zz, cc), dev(yy + NY - 1, xx, zz, cc)
    q2, qp, qm = (yy + 2) % NY, (yy + 1) % NY, (yy + NY - 1) % NY

    errors(q2)
    g = center_grad(q2).astype(bf16)
    pt[0, 0] = g[:half]
    pt[0, 1] = g[half:]
    send(pt.at[0, 0], rA2, ys_s.at[0], ys_r.at[0], yup)
    send(pt.at[0, 1], rB2, ys_s.at[1], ys_r.at[1], ydn)
    errors(qp)
    g = center_grad(qp)
    pt[1, 1] = g[half:].astype(bf16)
    send(pt.at[1, 1], rP.at[1], ys_s.at[2], ys_r.at[2], yup)
    gA = g[:half]
    landed(rA2, ys_r.at[0])
    pt[1, 0] = (gA + rA2[...].astype(f32)).astype(bf16)
    send(pt.at[1, 0], rP.at[0], ys_s.at[3], ys_r.at[3], yup)
    errors(qm)
    g = center_grad(qm)
    pt[2, 0] = g[:half].astype(bf16)
    send(pt.at[2, 0], rM.at[0], ys_s.at[4], ys_r.at[4], ydn)
    landed(rB2, ys_r.at[1])
    pt[2, 1] = (g[half:] + rB2[...].astype(f32)).astype(bf16)
    send(pt.at[2, 1], rM.at[1], ys_s.at[5], ys_r.at[5], ydn)
    errors(yy)
    pown[...] = center_grad(yy)

    @pl.loop(0, NZ)
    def _(z):
        lanes = pl.ds(pl.multiple_of(z * zrows, zrows), zrows)
        gt = nn_dot(wT[...], err[:, lanes])
        gx = gt.T
        lo, hi = gx[: zrows // 2], gx[zrows // 2:]
        gown[z] = jnp.where(cc == 0, lo, hi)
        goth[z] = jnp.where(cc == 0, hi, lo).astype(bf16)

    send(goth, pr, pr_s.at[0], pr_r.at[0], sib)

    def own_half(h):
        landed(rP.at[h], ys_r.at[3 - h])
        landed(rM.at[h], ys_r.at[4 + h])
        s = pown[pl.ds(h * half, half), :] + rP[h].astype(f32) + rM[h].astype(f32)
        gs[yy, h] = s.astype(bf16)
        send(gs.at[yy, h], gs.at[yy, h], yg_s.at[h], yg_r.at[h], yup)
        send(gs.at[yy, h], gs.at[yy, h], yg_s.at[2 + h], yg_r.at[2 + h], ydn)

    landed(pr, pr_r.at[0])

    @pl.loop(0, NZ)
    def _(z):
        h = gown[z] + pr[z].astype(f32)
        gown[z] = h
        for x in range(NX):
            xs[x, z] = h[x * rows:(x + 1) * rows].astype(bf16)

    for k in range(1, NX):
        send(xs.at[(xx + k) % NX], xr.at[k - 1], xs_s.at[k - 1], xs_r.at[k - 1], dev(yy, xx + k, zz, cc))

    own_half(0)
    own_half(1)

    ld_mom.wait()
    tile = 64
    stores = []

    def update(q, h, k):
        @pl.loop(0, half // tile)
        def _(i):
            r0 = pl.multiple_of(q * quart + h * half + i * tile, tile)
            r = pl.ds(r0, tile)
            g = gs[q, h, pl.ds(pl.multiple_of(i * tile, tile), tile), :].astype(f32)
            wb = cen[r, :]
            wf = wb.astype(f32)
            rn = 1.0 / wn[r, :]
            wu = wf * rn
            gw = (g - wu * jnp.sum(wu * g, axis=1, keepdims=True)) * rn
            live = (r0 // 128) < live_count
            v = mom[r, :]
            nv = jnp.where(live, momentum_rate * v + gw, v)
            nw = jnp.where(live, wf - learn_rate * nv, wf).astype(bf16)
            mom[r, :] = nv
            cen[r, :] = nw

        r = pl.ds(pl.multiple_of(q * quart + h * half, tile), half)
        for j, (src, dst) in enumerate(((cen, nw_hbm), (mom, nv_hbm))):
            c = pltpu.make_async_copy(src.at[r, :], dst.at[r, :], stsem.at[k, j])
            c.start()
            stores.append(c)

    update(yy, 0, 0)
    update(yy, 1, 1)

    landed(gs.at[qm, 0], yg_r.at[0])
    send(gs.at[qm, 0], gs.at[qm, 0], yg_s.at[4], yg_r.at[4], yup)
    landed(gs.at[qp, 1], yg_r.at[3])
    send(gs.at[qp, 1], gs.at[qp, 1], yg_s.at[5], yg_r.at[5], ydn)

    for k in range(1, NX):
        landed(xr.at[k - 1], xs_r.at[k - 1])
    for z in range(NZ):
        h = gown[z, pl.ds(xrow, rows), :]
        for k in range(1, NX):
            h = h + xr[k - 1, z].astype(f32)
        gown[z, pl.ds(xrow, rows), :] = h
        zs[z] = h.astype(bf16)
    for dz in range(1, NZ):
        send(zs.at[(zz + dz) % NZ], zr.at[dz - 1], zs_s.at[dz - 1], zs_r.at[dz - 1], dev(yy, xx, zz + dz, cc))

    landed(gs.at[qm, 1], yg_r.at[1])
    landed(gs.at[qp, 0], yg_r.at[2])
    update(qm, 0, 2)
    update(qm, 1, 3)
    update(qp, 0, 4)
    update(qp, 1, 5)

    gx = gown[zz, pl.ds(xrow, rows), :]
    for dz in range(1, NZ):
        landed(zr.at[dz - 1], zs_r.at[dz - 1])
        gx = gx + zr[dz - 1].astype(f32)
    eg_ref[...] = (gx - xu * jnp.sum(xu * gx, axis=1, keepdims=True)) / xn
    pos = pos_last()
    all_loss = jnp.log(scale / inv[...]) - (scale * pos - scale * margin)
    inv[...] = all_loss
    line = inv[pl.ds(zz, 1), :]
    mine = jnp.zeros((1, rows), f32)
    for c in range(NC):
        for x in range(NX):
            at = (c * NX + x) * rows
            here = jnp.logical_and(cc == c, xx == x)
            mine = jnp.where(here, line[:, at:at + rows], mine)
    loss_ref[...] = mine

    landed(gs.at[q2, 0], yg_r.at[4])
    update(q2, 0, 6)
    landed(gs.at[q2, 1], yg_r.at[5])
    update(q2, 1, 7)

    for c in sends:
        c.wait_send()
    for c in stores:
        c.wait()


def on_device(embeddings, labels, centers, momentum, block_list, counts):
    rows, width = embeddings.shape
    slots, blk, _ = centers.shape
    cols = slots * blk
    zrows = NC * NX * rows
    group = NZ * zrows
    quart = cols // NY
    half = quart // 2
    vm, dma = pltpu.VMEM, pltpu.SemaphoreType.DMA
    npeer = NX * NC - 1
    scratch = [
        vm((cols, width), bf16),
        vm((cols, width), f32),
        vm((cols, width), bf16),
        vm((width, cols), bf16),
        vm((cols, 1), f32),
        vm((NZ, NC, NX * rows, width), bf16),
        vm((NX * NC, 1, 128), i32),
        vm((NZ, NC, 1, 128), i32),
        vm((NZ, 1, zrows), i32),
        vm((cols, group), f32),
        vm((cols, group), bf16),
        vm((NZ, zrows), f32),
        vm((NZ, zrows), f32),
        vm((npeer, NZ, zrows), f32),
        vm((NZ, NZ, zrows), f32),
        vm((npeer, NZ, zrows), f32),
        vm((NZ, NZ, zrows), f32),
        vm((NZ, zrows), f32),
        vm((NY - 1, 2, half, width), bf16),
        vm((quart, width), f32),
        vm((NY, 2, half, width), bf16),
        vm((half, width), bf16),
        vm((half, width), bf16),
        vm((2, half, width), bf16),
        vm((2, half, width), bf16),
        vm((NZ, NX * rows, width), f32),
        vm((NZ, NX * rows, width), bf16),
        vm((NZ, NX * rows, width), bf16),
        vm((NX, NZ, rows, width), bf16),
        vm((NX - 1, NZ, rows, width), bf16),
        vm((NZ, rows, width), bf16),
        vm((NZ - 1, rows, width), bf16),
        dma((2,)), dma((8, 2)),
        dma((NX - 1,)), dma((NX - 1,)), dma((npeer,)), dma((npeer,)), dma((NZ - 1,)), dma((NZ - 1,)),
        dma((2, NZ // 2)), dma((2, NZ // 2)), dma((NZ + 1,)), dma((NZ + 1,)),
        dma((npeer,)), dma((npeer,)), dma((NZ - 1,)), dma((NZ - 1,)),
        dma((npeer,)), dma((npeer,)), dma((NZ - 1,)), dma((NZ - 1,)),
        dma((6,)), dma((6,)), dma((6,)), dma((6,)), dma((1,)), dma((1,)),
        dma((NX - 1,)), dma((NX - 1,)), dma((NZ - 1,)), dma((NZ - 1,)),
    ]
    vmem = pl.BlockSpec(memory_space=pltpu.VMEM)
    smem = pl.BlockSpec(memory_space=pltpu.SMEM)
    hbm = pl.BlockSpec(memory_space=pl.ANY)
    loss, eg, nw, nv = pl.pallas_call(
        kernel,
        out_shape=(
            jax.ShapeDtypeStruct((1, rows), f32),
            jax.ShapeDtypeStruct((rows, width), f32),
            jax.ShapeDtypeStruct((cols, width), bf16),
            jax.ShapeDtypeStruct((cols, width), f32),
        ),
        in_specs=[vmem, vmem, smem, smem, hbm, hbm],
        out_specs=(vmem, vmem, hbm, hbm),
        scratch_shapes=scratch,
        compiler_params=pltpu.CompilerParams(
            collective_id=0, has_side_effects=True, vmem_limit_bytes=62 * 1024 * 1024
        ),
        name="margin_step",
    )(
        embeddings,
        jnp.tile(labels, 128 // rows).reshape(1, 128),
        block_list,
        counts,
        centers.reshape(cols, width),
        momentum.reshape(cols, width),
    )
    return (
        loss.reshape(rows),
        eg,
        nw.reshape(centers.shape),
        nv.reshape(momentum.shape),
    )


def solution(mesh):
    return jax.shard_map(
        on_device,
        mesh=mesh,
        in_specs=(
            P(("dp", "center"), None),
            P(("dp", "center")),
            P("center", None, None),
            P("center", None, None),
            P("center"),
            P("center"),
        ),
        out_specs=(
            P(("dp", "center")),
            P(("dp", "center"), None),
            P("center", None, None),
            P("center", None, None),
        ),
        check_vma=False,
    )
```

time: 724 us -> 101 us (0.14)
  blocking collectives: 264 us -> 0 us
  waiting for transfers between devices: 253 us -> 0 us
  local copies, waits for them, and re-layouts: 110 us -> 8.32 us
  Pallas kernels: 0 us -> 91.1 us
  other arithmetic: 51 us -> 0 us
  matrix products: 27.4 us -> 0 us
  between operations: 15.2 us -> 1.3 us
    psum x1 -> x0, blocking collectives: 243 us -> none  [on_device(): lax.psum((part_total.reshape(group_count), part_pos.reshape(group_count))...]
    psum x2 -> x0, waiting for transfers between devices: 219 us -> none  [the longest x1 184 us: on_device(): lax.psum(jnp.dot(err_bf, w_bf, preferred_element_type=jnp.float32), 'cent...]
    pallas_call x0 -> x1, Pallas kernels: none -> 91.1 us  [on_device(): pl.pallas_call(kernel, out_shape=(jax.ShapeDtypeStruct((1, rows), f32), j...]
    dynamic_slice x8 -> x0, local copies, waits for them, and re-layouts: 60.9 us -> none  [on_device(): lax.map(first_pass, (group_x.reshape(block_total, step_rows, width), hit_...]
    all_gather x1 -> x0, waiting for transfers between devices: 33.9 us -> none  [on_device(): lax.all_gather(x_bf, 'center', axis=0, tiled=True)]
    convert_element_type x5 -> x0, other arithmetic: 29.1 us -> none  [the longest x2 20 us: on_device(): (logit_scale * (exp_z / total[:, None] - hit_float)).astype(jnp.bfloat16)]
    dot_general x6 -> x0, matrix products: 27.4 us -> none  [the longest x4 17.9 us: first_pass(): lax.dot_general(x_block, w_bf, (((1,), (1,)), ((), ())), preferred_elemen...]
    unnamed x1 -> x0, blocking collectives: 21.1 us -> none
  transfers between devices with their start and end apart: 3 -> 0, of which waited for: 3 -> 0; matrix products, arithmetic and copies ran while one was open for 8% -> 0% of each run, Pallas kernels for 0% -> 0%
where the time goes in v1:
time: 101 us
  Pallas kernels  91.1 us (90%)
  local copies, waits for them, and re-layouts  8.32 us (8%)
  between operations  1.3 us (1%)
    pallas_call x1, Pallas kernels, on_device(): pl.pallas_call(kernel, out_shape=(jax.ShapeDtypeStruct((1, rows), f32), j...  91.1 us
    unnamed x6, local copies, waits for them, and re-layouts  7.07 us

profile of v1, /device:TPU:1, one launch (start us, length us, event | category | flops | bytes accessed | tf_op | source)
XLA Modules:
  0.0 100.7 jit_solution(16531036788235011654)
XLA Ops:
  1.3 0.7 tile.2
  1.9 0.6 reshape_tile.3.lab_ref
  2.5 91.1 %margin_step.1 = (f32[1,32]{1,0:T(1,128)}, f32[32,512]{1,0:T(8,128)}, bf16[1536,512]{1,0:T(8,128)(2,1)}, f32[1536,512]{1,0:T(8,128)}) custom-call(bf16[32,512]{1,0:T(8,128)(2,1)} %emb_ref.1, s32[1,128]{1,0:T(1,128)} %reshape_tile.3.lab_ref, s32[12]{0:T(128)} %ids_ref.1, s32[1]{0:T(128)S(6)} %copy.14.cnt_ref, bf16[1536,512]{1,0:T(8,128)(2,1)} %bitcast.8, ...), custom_call_target="tpu_custom_call" | custom-call | tf_op jit(solution)/shard_map/margin_step/pallas_call | solution.py:462
  93.6 0.0 copy-start
  93.6 1.3 %copy.15 = f32[32]{0:T(128)} copy(f32[32]{0:T(128)} %bitcast.9) | data formatting | bytes 256
  94.9 1.5 %copy.16 = f32[32,512]{1,0:T(8,128)} copy(f32[32,512]{1,0:T(8,128)} %get-tuple-element.17) | data formatting | bytes 131072
  96.4 2.7 %copy.17 = bf16[12,128,512]{2,1,0:T(8,128)(2,1)} copy(bf16[12,128,512]{2,1,0:T(8,128)(2,1)} %bitcast.7) | data formatting | bytes 3145728
  99.0 0.0 copy-done
  99.0 1.7 %copy.18 = f32[12,128,512]{2,1,0:T(8,128)} copy(f32[12,128,512]{2,1,0:T(8,128)S(1)} %bitcast.5) | data formatting | bytes 6291456
Async XLA Ops:
  93.6 5.4 %copy-start = (f32[1536,512]{1,0:T(8,128)S(1)}, f32[1536,512]{1,0:T(8,128)}, u32[]{:S(2)}) copy-start(f32[1536,512]{1,0:T(8,128)} %get-tuple-element.11) | copy-start | bytes 9437188

commit v2 on v1

v2 whole, which is shorter than its diff:
```python
import math

import jax
import jax.numpy as jnp
from jax import lax
from jax.experimental import pallas as pl
from jax.experimental.pallas import tpu as pltpu
from jax.sharding import PartitionSpec as P

MESH = pl.DeviceIdType.MESH
NX, NZ, NC, NY = 4, 8, 2, 4
f32, bf16, i32 = jnp.float32, jnp.bfloat16, jnp.int32

scale = 64.0
margin = 0.35
momentum_rate = 0.9
learn_rate = 0.1
tiny_eps = 1e-06
log2e = math.log2(math.e)
dead_bias = -1e30


def nt_dot(a, b):
    return lax.dot_general(a, b, (((1,), (1,)), ((), ())), preferred_element_type=f32)


def nn_dot(a, b):
    return lax.dot_general(a, b, (((1,), (0,)), ((), ())), preferred_element_type=f32)


def kernel(
    emb_ref, lab_ref, ids_ref, cnt_ref, cen_hbm, mom_hbm,
    loss_ref, eg_ref, nw_hbm, nv_hbm,
    cen, mom, wbf, wT, wn, xg, labs, labz, tgt, ez, err, tp, pp, t1, t2, p1, p2, inv,
    pt, pf, gs, r2, rP, rM,
    gown, goth, pr, xs, xr, zs, zr,
    ldsem, stsem,
    xa_s, xa_r, la_s, la_r, lz_s, lz_r, zg_s, zg_r, sb_s, sb_r,
    t1_s, t1_r, t2_s, t2_r, p1_s, p1_r, p2_s, p2_r,
    ys_s, ys_r, yg_s, yg_r, pr_s, pr_r, xs_s, xs_r, zs_s, zs_r,
):
    rows = emb_ref.shape[0]
    width = emb_ref.shape[1]
    cols = cen.shape[0]
    quart = cols // NY
    piece = quart // 4
    slots = cols // 128
    zrows = NC * NX * rows
    yy = lax.axis_index("dp")
    ce = lax.axis_index("center")
    xx = ce // (NZ * NC)
    zz = (ce // NC) % NZ
    cc = ce % NC

    def dev(y, x, z, c):
        return (y % NY, ((x % NX) * NZ + z % NZ) * NC + c)

    def copy(src, dst, ssem, rsem, to):
        return pltpu.make_async_remote_copy(
            src_ref=src, dst_ref=dst, send_sem=ssem, recv_sem=rsem, device_id=to, device_id_type=MESH
        )

    me = (yy, ce)
    sib = dev(yy, xx, zz, 1 - cc)

    def landed(dst, rsem):
        copy(dst, dst, rsem, rsem, sib).wait_recv()

    xc_peers = [(dx, dc) for dx in range(NX) for dc in range(NC) if (dx, dc) != (0, 0)]
    sends = []

    def send(src, dst, ssem, rsem, to):
        c = copy(src, dst, ssem, rsem, to)
        c.start()
        sends.append(c)

    ld_cen = pltpu.make_async_copy(cen_hbm, cen, ldsem.at[0])
    ld_mom = pltpu.make_async_copy(mom_hbm, mom, ldsem.at[1])
    ld_cen.start()
    ld_mom.start()
    barrier = pltpu.get_barrier_semaphore()
    greet = [dev(yy, xx + dx, zz, (cc + dc) % NC) for dx, dc in xc_peers]
    greet += [dev(yy, xx, zz + dz, cc) for dz in range(1, NZ)]
    greet += [dev(yy + 1, xx, zz, cc), dev(yy + NY - 1, xx, zz, cc)]
    for d in greet:
        pl.semaphore_signal(barrier, inc=1, device_id=d, device_id_type=MESH)

    xf = emb_ref[...].astype(f32)
    xn = jnp.sqrt(jnp.sum(xf * xf, axis=1, keepdims=True) + tiny_eps)
    xu = xf / xn
    xrow = pl.multiple_of(xx * rows, rows)
    xg[zz, cc, pl.ds(xrow, rows), :] = xu.astype(bf16)
    lab = jnp.concatenate([lab_ref[...]] * NX, axis=1)
    lane = lax.broadcasted_iota(i32, (1, 128), 1)
    labs[0] = jnp.where(lane // rows == xx, lab, 0)
    pl.semaphore_wait(barrier, len(greet))

    def block(dz, dx):
        return xg.at[(zz + NZ - dz) % NZ, cc, pl.ds(pl.multiple_of(((xx + NX - dx) % NX) * rows, rows), rows), :]

    def along_x(dz):
        for k in (1, 3, 2):
            send(block(dz, 0), block(dz, 0), xa_s.at[dz, k - 1], xa_r.at[dz, k - 1], dev(yy, xx + k, zz, cc))

    for dz in (1, 7, 2, 6, 3, 5, 4):
        send(block(0, 0), block(0, 0), zg_s.at[dz - 1], zg_r.at[dz - 1], dev(yy, xx, zz + dz, cc))
    along_x(0)
    for k, (dx, dc) in enumerate(xc_peers):
        send(labs.at[0], labs.at[dx * NC + dc], la_s.at[k], la_r.at[k], dev(yy, xx + dx, zz, (cc + dc) % NC))

    ld_cen.wait()

    @pl.loop(0, slots)
    def _(s):
        r = pl.ds(pl.multiple_of(s * 128, 128), 128)
        wf = cen[r, :].astype(f32)
        n = jnp.sqrt(jnp.sum(wf * wf, axis=1, keepdims=True) + tiny_eps)
        wn[r, :] = n
        wbf[r, :] = (wf * (1.0 / n)).astype(bf16)

    def forward(dz):
        landed(block(dz, 0), zg_r.at[dz - 1])
        along_x(dz)

    def share(dz):
        for k in (1, 3, 2):
            landed(block(dz, k), xa_r.at[dz, k - 1])
        p = xg.at[(zz + NZ - dz) % NZ, cc]
        send(p, p, sb_s.at[dz], sb_r.at[dz], sib)

    forward(1)
    forward(7)
    share(0)

    for k, (dx, dc) in enumerate(xc_peers):
        landed(labs.at[dx * NC + dc], la_r.at[k])
    same, other = labs[0], labs[1]
    for dx in range(1, NX):
        same = same + labs[dx * NC]
        other = other + labs[dx * NC + 1]
    labz[zz, 0] = jnp.where(cc == 0, same, other)
    labz[zz, 1] = jnp.where(cc == 0, other, same)
    for dz in (1, 7, 2, 6, 3, 5, 4):
        send(labz.at[zz], labz.at[zz], lz_s.at[dz - 1], lz_r.at[dz - 1], dev(yy, xx, zz + dz, cc))

    def targets(z):
        lb = jnp.concatenate([labz[z, 0], labz[z, 1]], axis=1)
        blk_id = lb // 128
        t = jnp.full(lb.shape, -1, i32)
        for s in range(slots):
            t = jnp.where(blk_id == ids_ref[s], s * 128 + lb % 128, t)
        tgt[z] = t
        return t

    live_count = cnt_ref[0]
    k2 = scale * log2e
    hit_bias = -scale * margin * log2e
    group = 4 if slots % 4 == 0 else 1

    def first_pass(dz):
        z = (zz + NZ - dz) % NZ
        landed(xg.at[z, 1 - cc], sb_r.at[dz])
        if dz:
            landed(labz.at[z], lz_r.at[dz - 1])
        xc = xg[z].reshape(zrows, width)
        tz = targets(z)
        iota = lax.broadcasted_iota(i32, (128, zrows), 0)
        lanes = pl.ds(pl.multiple_of(z * zrows, zrows), zrows)

        def body(g, carry):
            tot, pos = carry
            r0 = pl.multiple_of(g * (group * 128), 128)
            s = nt_dot(wbf[pl.ds(r0, group * 128), :], xc)
            for u in range(group):
                slot = g * group + u
                su = s[u * 128:(u + 1) * 128]
                hit = iota == (tz - slot * 128)
                bias = jnp.where(slot < live_count, 0.0, dead_bias)
                e = jnp.exp2(su * k2 + jnp.where(hit, hit_bias, bias))
                ez[pl.ds(r0 + u * 128, 128), lanes] = e
                tot = tot + jnp.sum(e, axis=0, keepdims=True)
                pos = pos + jnp.sum(jnp.where(hit, su, 0.0), axis=0, keepdims=True)
            return tot, pos

        zero = jnp.zeros((1, zrows), f32)
        tot, pos = lax.fori_loop(0, slots // group, body, (zero, zero))
        tp[pl.ds(z, 1), :] = tot
        pp[pl.ds(z, 1), :] = pos

    forward(2)
    forward(6)
    first_pass(0)
    share(1)
    share(7)
    forward(3)
    forward(5)
    forward(4)
    first_pass(1)
    first_pass(7)
    share(2)
    share(6)
    first_pass(2)
    first_pass(6)
    share(3)
    share(5)
    share(4)
    first_pass(3)
    first_pass(5)

    @pl.loop(0, slots)
    def _(s):
        c0 = pl.multiple_of(s * 128, 128)
        wT[:, pl.ds(c0, 128)] = wbf[pl.ds(c0, 128), :].T

    first_pass(4)

    def reduce_plane(part, first, second, s1, r1, s2, r2):
        for k, (dx, dc) in enumerate(xc_peers):
            send(part, first.at[k], s1.at[k], r1.at[k], dev(yy, xx + dx, zz, (cc + dc) % NC))

        def middle():
            acc = part[...]
            for k in range(len(xc_peers)):
                landed(first.at[k], r1.at[k])
                acc = acc + first[k]
            second[0] = acc
            for dz in range(1, NZ):
                send(second.at[0], second.at[dz], s2.at[dz - 1], r2.at[dz - 1], dev(yy, xx, zz + dz, cc))

        def last():
            acc = second[0]
            for dz in range(1, NZ):
                landed(second.at[dz], r2.at[dz - 1])
                acc = acc + second[dz]
            return acc

        return middle, last

    tot_mid, tot_last = reduce_plane(tp, t1, t2, t1_s, t1_r, t2_s, t2_r)
    tot_mid()
    total = tot_last()
    inv[...] = scale / total

    def errors(q):
        @pl.loop(0, NZ)
        def _(z):
            lanes = pl.ds(pl.multiple_of(z * zrows, zrows), zrows)
            iota = lax.broadcasted_iota(i32, (128, zrows), 0)
            iz = inv[pl.ds(z, 1), :]
            tz = tgt[z]
            for u in range(quart // 128):
                r0 = pl.multiple_of(q * quart + u * 128, 128)
                hit = iota == (tz - r0)
                e = ez[pl.ds(r0, 128), lanes] * iz - jnp.where(hit, scale, 0.0)
                err[pl.ds(r0, 128), lanes] = e.astype(bf16)

    def center_grad(q):
        r0 = pl.multiple_of(q * quart, 128)
        return nn_dot(err[pl.ds(r0, quart), :], xg[...].reshape(NZ * zrows, width))

    yup, ydn = dev(yy + 1, xx, zz, cc), dev(yy + NY - 1, xx, zz, cc)
    q2, qp, qm = (yy + 2) % NY, (yy + 1) % NY, (yy + NY - 1) % NY

    def to_y(src, dst, k, to):
        send(src, dst, ys_s.at[k], ys_r.at[k], to)

    def keep(q, slot):
        g = center_grad(q)
        for p in range(4):
            pt[slot, p] = g[p * piece:(p + 1) * piece].astype(bf16)
        return g

    errors(q2)
    keep(q2, 0)
    for n in range(2):
        to_y(pt.at[0, n], r2.at[n], n, yup)
        to_y(pt.at[0, 2 + n], r2.at[2 + n], 2 + n, ydn)
    errors(qp)
    pf[0] = center_grad(qp)
    for n in range(2):
        pt[1, 2 + n] = pf[0, pl.ds((2 + n) * piece, piece), :].astype(bf16)
    to_y(pt.at[1, 2], rP.at[2], 4, yup)
    errors(qm)
    pf[1] = center_grad(qm)
    for n in range(2):
        pt[2, n] = pf[1, pl.ds(n * piece, piece), :].astype(bf16)
    to_y(pt.at[2, 0], rM.at[0], 5, ydn)
    errors(yy)

    def merge(n):
        landed(r2.at[n], ys_r.at[n])
        pt[1, n] = (pf[0, pl.ds(n * piece, piece), :] + r2[n].astype(f32)).astype(bf16)
        to_y(pt.at[1, n], rP.at[n], 6 + n, yup)
        landed(r2.at[2 + n], ys_r.at[2 + n])
        pt[2, 2 + n] = (pf[1, pl.ds((2 + n) * piece, piece), :] + r2[2 + n].astype(f32)).astype(bf16)
        to_y(pt.at[2, 2 + n], rM.at[2 + n], 8 + n, ydn)

    def own(n):
        for p in (n, 2 + n):
            landed(rP.at[p], ys_r.at[(6 + n) if p < 2 else (4 if n == 0 else 10)])
            landed(rM.at[p], ys_r.at[(8 + n) if p >= 2 else (5 if n == 0 else 11)])
            s = pf[2, pl.ds(p * piece, piece), :] + rP[p].astype(f32) + rM[p].astype(f32)
            gs[yy, p] = s.astype(bf16)
        for p, q in ((n, 2 + n),):
            send(gs.at[yy, p], gs.at[yy, p], yg_s.at[0, p], yg_r.at[0, p], yup)
            send(gs.at[yy, q], gs.at[yy, q], yg_s.at[1, q], yg_r.at[1, q], ydn)
            send(gs.at[yy, q], gs.at[yy, q], yg_s.at[0, q], yg_r.at[0, q], yup)
            send(gs.at[yy, p], gs.at[yy, p], yg_s.at[1, p], yg_r.at[1, p], ydn)

    def onward(n):
        landed(gs.at[qm, n], yg_r.at[0, n])
        send(gs.at[qm, n], gs.at[qm, n], yg_s.at[2, n], yg_r.at[2, n], yup)
        landed(gs.at[qp, 2 + n], yg_r.at[1, 2 + n])
        send(gs.at[qp, 2 + n], gs.at[qp, 2 + n], yg_s.at[2, 2 + n], yg_r.at[2, 2 + n], ydn)

    group2 = NZ // 2

    def row_grad(lo, hi):
        @pl.loop(lo, hi)
        def _(i):
            z = (zz + NZ // 2 + i) % NZ
            lanes = pl.ds(pl.multiple_of(z * zrows, zrows), zrows)
            gx = nn_dot(wT[...], err[:, lanes]).T
            a, b = gx[: zrows // 2], gx[zrows // 2:]
            gown[i] = jnp.where(cc == 0, a, b)
            goth[i] = jnp.where(cc == 0, b, a).astype(bf16)

    def pair(g):
        part = pl.ds(g * group2, group2)
        send(goth.at[part], pr.at[part], pr_s.at[g], pr_r.at[g], sib)

    def rows_x(g):
        part = pl.ds(g * group2, group2)
        landed(pr.at[part], pr_r.at[g])

        @pl.loop(0, group2)
        def _(n):
            i = g * group2 + n
            h = gown[i] + pr[i].astype(f32)
            gown[i] = h
            for x in range(NX):
                xs[g, x, n] = h[x * rows:(x + 1) * rows].astype(bf16)

        for k in (1, 3, 2):
            send(xs.at[g, (xx + k) % NX], xr.at[g, k - 1], xs_s.at[g, k - 1], xs_r.at[g, k - 1], dev(yy, xx + k, zz, cc))

    def rows_z(g):
        for k in range(1, NX):
            landed(xr.at[g, k - 1], xs_r.at[g, k - 1])
        for n in range(group2):
            i = g * group2 + n
            dz = (NZ // 2 + i) % NZ
            h = gown[i, pl.ds(xrow, rows), :]
            for k in range(1, NX):
                h = h + xr[g, k - 1, n].astype(f32)
            if dz == 0:
                gown[i, pl.ds(xrow, rows), :] = h
            else:
                zs[i] = h.astype(bf16)
                send(zs.at[i], zr.at[dz - 1], zs_s.at[dz - 1], zs_r.at[dz - 1], dev(yy, xx, zz + dz, cc))

    pos_mid, pos_last = reduce_plane(pp, p1, p2, p1_s, p1_r, p2_s, p2_r)
    merge(0)
    to_y(pt.at[1, 3], rP.at[3], 10, yup)
    to_y(pt.at[2, 1], rM.at[1], 11, ydn)
    row_grad(0, group2)
    pair(0)
    merge(1)
    pf[2] = center_grad(yy)
    rows_x(0)
    row_grad(group2, group2 + 2)
    own(0)
    row_grad(group2 + 2, NZ)
    pair(1)
    pos_mid()
    own(1)
    rows_x(1)

    ld_mom.wait()
    tile = 32
    stores = []

    def update(q, p0, np, k):
        base = q * quart + p0 * piece

        @pl.loop(0, np * piece // tile)
        def _(i):
            at = pl.multiple_of(i * tile, tile)
            r0 = pl.multiple_of(base + at, tile)
            r = pl.ds(r0, tile)
            g = gs[q, p0 + at // piece, pl.ds(pl.multiple_of(at % piece, tile), tile), :].astype(f32)
            wf = cen[r, :].astype(f32)
            rn = 1.0 / wn[r, :]
            wu = wf * rn
            gw = (g - wu * jnp.sum(wu * g, axis=1, keepdims=True)) * rn
            live = (r0 // 128) < live_count
            v = mom[r, :]
            nv = jnp.where(live, momentum_rate * v + gw, v)
            nw = jnp.where(live, wf - learn_rate * nv, wf).astype(bf16)
            mom[r, :] = nv
            cen[r, :] = nw

        r = pl.ds(pl.multiple_of(base, tile), np * piece)
        for j, (src, dst) in enumerate(((cen, nw_hbm), (mom, nv_hbm))):
            c = pltpu.make_async_copy(src.at[r, :], dst.at[r, :], stsem.at[k, j])
            c.start()
            stores.append(c)

    update(yy, 0, 4, 0)
    onward(0)
    rows_z(0)
    onward(1)
    rows_z(1)
    for n in range(2):
        landed(gs.at[qm, 2 + n], yg_r.at[0, 2 + n])
        landed(gs.at[qp, n], yg_r.at[1, n])
    update(qm, 0, 4, 1)
    update(qp, 0, 4, 2)

    gx = gown[NZ // 2, pl.ds(xrow, rows), :]
    for dz in range(1, NZ):
        landed(zr.at[dz - 1], zs_r.at[dz - 1])
        gx = gx + zr[dz - 1].astype(f32)
    eg_ref[...] = (gx - xu * jnp.sum(xu * gx, axis=1, keepdims=True)) / xn
    pos = pos_last()
    all_loss = jnp.log(scale / inv[...]) - (scale * pos - scale * margin)
    inv[...] = all_loss
    line = inv[pl.ds(zz, 1), :]
    mine = jnp.zeros((1, rows), f32)
    for c in range(NC):
        for x in range(NX):
            at = (c * NX + x) * rows
            here = jnp.logical_and(cc == c, xx == x)
            mine = jnp.where(here, line[:, at:at + rows], mine)
    loss_ref[...] = mine

    for n in range(2):
        landed(gs.at[q2, n], yg_r.at[2, n])
        landed(gs.at[q2, 2 + n], yg_r.at[2, 2 + n])
    update(q2, 0, 4, 3)

    for c in sends:
        c.wait_send()
    for c in stores:
        c.wait()


def on_device(embeddings, labels, centers, momentum, block_list, counts):
    rows, width = embeddings.shape
    slots, blk, _ = centers.shape
    cols = slots * blk
    zrows = NC * NX * rows
    group = NZ * zrows
    quart = cols // NY
    piece = quart // 4
    vm, dma = pltpu.VMEM, pltpu.SemaphoreType.DMA
    npeer = NX * NC - 1
    scratch = [
        vm((cols, width), bf16),
        vm((cols, width), f32),
        vm((cols, width), bf16),
        vm((width, cols), bf16),
        vm((cols, 1), f32),
        vm((NZ, NC, NX * rows, width), bf16),
        vm((NX * NC, 1, 128), i32),
        vm((NZ, NC, 1, 128), i32),
        vm((NZ, 1, zrows), i32),
        vm((cols, group), f32),
        vm((cols, group), bf16),
        vm((NZ, zrows), f32),
        vm((NZ, zrows), f32),
        vm((npeer, NZ, zrows), f32),
        vm((NZ, NZ, zrows), f32),
        vm((npeer, NZ, zrows), f32),
        vm((NZ, NZ, zrows), f32),
        vm((NZ, zrows), f32),
        vm((3, 4, piece, width), bf16),
        vm((3, quart, width), f32),
        vm((NY, 4, piece, width), bf16),
        vm((4, piece, width), bf16),
        vm((4, piece, width), bf16),
        vm((4, piece, width), bf16),
        vm((NZ, NX * rows, width), f32),
        vm((NZ, NX * rows, width), bf16),
        vm((NZ, NX * rows, width), bf16),
        vm((2, NX, NZ // 2, rows, width), bf16),
        vm((2, NX - 1, NZ // 2, rows, width), bf16),
        vm((NZ, rows, width), bf16),
        vm((NZ - 1, rows, width), bf16),
        dma((2,)), dma((4, 2)),
        dma((NZ, NX - 1)), dma((NZ, NX - 1)), dma((npeer,)), dma((npeer,)), dma((NZ - 1,)), dma((NZ - 1,)),
        dma((NZ - 1,)), dma((NZ - 1,)), dma((NZ,)), dma((NZ,)),
        dma((npeer,)), dma((npeer,)), dma((NZ - 1,)), dma((NZ - 1,)),
        dma((npeer,)), dma((npeer,)), dma((NZ - 1,)), dma((NZ - 1,)),
        dma((12,)), dma((12,)), dma((3, 4)), dma((3, 4)), dma((2,)), dma((2,)),
        dma((2, NX - 1)), dma((2, NX - 1)), dma((NZ - 1,)), dma((NZ - 1,)),
    ]
    vmem = pl.BlockSpec(memory_space=pltpu.VMEM)
    smem = pl.BlockSpec(memory_space=pltpu.SMEM)
    hbm = pl.BlockSpec(memory_space=pl.ANY)
    loss, eg, nw, nv = pl.pallas_call(
        kernel,
        out_shape=(
            jax.ShapeDtypeStruct((1, rows), f32),
            jax.ShapeDtypeStruct((rows, width), f32),
            jax.ShapeDtypeStruct((cols, width), bf16),
            jax.ShapeDtypeStruct((cols, width), f32),
        ),
        in_specs=[vmem, vmem, smem, smem, hbm, hbm],
        out_specs=(vmem, vmem, hbm, hbm),
        scratch_shapes=scratch,
        compiler_params=pltpu.CompilerParams(
            collective_id=0, has_side_effects=True, vmem_limit_bytes=62 * 1024 * 1024
        ),
        name="margin_step",
    )(
        embeddings,
        labels.reshape(1, rows),
        block_list,
        counts,
        centers.reshape(cols, width),
        momentum.reshape(cols, width),
    )
    return (
        loss.reshape(rows),
        eg,
        nw.reshape(centers.shape),
        nv.reshape(momentum.shape),
    )


def solution(mesh):
    return jax.shard_map(
        on_device,
        mesh=mesh,
        in_specs=(
            P(("dp", "center"), None),
            P(("dp", "center")),
            P("center", None, None),
            P("center", None, None),
            P("center"),
            P("center"),
        ),
        out_specs=(
            P(("dp", "center")),
            P(("dp", "center"), None),
            P("center", None, None),
            P("center", None, None),
        ),
        check_vma=False,
    )
```

time: 101 us -> 86.7 us (0.86)
  Pallas kernels: 91.1 us -> 77.8 us
  local copies, waits for them, and re-layouts: 8.32 us -> 7.07 us
    pallas_call x1, Pallas kernels: 91.1 us -> 77.8 us  [on_device(): pl.pallas_call(kernel, out_shape=(jax.ShapeDtypeStruct((1, rows), f32), j...]
    another operation x2 -> x0, local copies, waits for them, and re-layouts: 1.25 us -> none  [on_device(): jnp.tile(labels, 128 // rows).reshape(1, 128)]
where the time goes in v2:
time: 86.7 us; the launch traced here: 86.1 us
  Pallas kernels  77.8 us (90%)
  local copies, waits for them, and re-layouts  7.07 us (8%)
  between operations  1.3 us (1%)
    pallas_call x1, Pallas kernels, on_device(): pl.pallas_call(kernel, out_shape=(jax.ShapeDtypeStruct((1, rows), f32), j...  77.8 us
    unnamed x6, local copies, waits for them, and re-layouts  7.07 us

profile of v2, /device:TPU:1, one launch (start us, length us, event | category | flops | bytes accessed | tf_op | source)
XLA Modules:
  0.0 86.1 jit_solution(10452610789358037868)
XLA Ops:
  1.3 77.8 %margin_step.1 = (f32[1,32]{1,0:T(1,128)}, f32[32,512]{1,0:T(8,128)}, bf16[1536,512]{1,0:T(8,128)(2,1)}, f32[1536,512]{1,0:T(8,128)}) custom-call(bf16[32,512]{1,0:T(8,128)(2,1)} %emb_ref.1, s32[1,32]{1,0:T(1,128)} %bitcast.10, s32[12]{0:T(128)} %ids_ref.1, s32[1]{0:T(128)S(6)} %copy.14.cnt_ref, bf16[1536,512]{1,0:T(8,128)(2,1)} %bitcast.9, f32[1536,512]{1,0:T(8,128)} %bitcast.7), custom_call_target="tpu_custom_call" | custom-call | tf_op jit(solution)/shard_map/margin_step/pallas_call | solution.py:501
  79.1 0.0 copy-start
  79.1 1.3 %copy.15 = f32[32]{0:T(128)} copy(f32[32]{0:T(128)} %bitcast.11) | data formatting | bytes 256
  80.3 1.5 %copy.16 = f32[32,512]{1,0:T(8,128)} copy(f32[32,512]{1,0:T(8,128)} %get-tuple-element.17) | data formatting | bytes 131072
  81.8 2.7 %copy.17 = bf16[12,128,512]{2,1,0:T(8,128)(2,1)} copy(bf16[12,128,512]{2,1,0:T(8,128)(2,1)} %bitcast.8) | data formatting | bytes 3145728
  84.5 0.0 copy-done
  84.5 1.7 %copy.18 = f32[12,128,512]{2,1,0:T(8,128)} copy(f32[12,128,512]{2,1,0:T(8,128)S(1)} %bitcast.6) | data formatting | bytes 6291456
Async XLA Ops:
  79.1 5.4 %copy-start = (f32[1536,512]{1,0:T(8,128)S(1)}, f32[1536,512]{1,0:T(8,128)}, u32[]{:S(2)}) copy-start(f32[1536,512]{1,0:T(8,128)} %get-tuple-element.11) | copy-start | bytes 9437188

commit v3 on v2

--- a/solution.py
+++ b/solution.py
@@ -35,7 +35,7 @@
     pt, pf, gs, r2, rP, rM,
     gown, goth, pr, xs, xr, zs, zr,
     ldsem, stsem,
-    xa_s, xa_r, la_s, la_r, lz_s, lz_r, zg_s, zg_r, sb_s, sb_r,
+    xa_s, xa_r, xz_s, xz_r, la_s, la_r, lz_s, lz_r, zg_s, zg_r, sb_s, sb_r,
     t1_s, t1_r, t2_s, t2_r, p1_s, p1_r, p2_s, p2_r,
     ys_s, ys_r, yg_s, yg_r, pr_s, pr_r, xs_s, xs_r, zs_s, zs_r,
 ):
@@ -102,9 +102,13 @@
         for k in (1, 3, 2):
             send(block(dz, 0), block(dz, 0), xa_s.at[dz, k - 1], xa_r.at[dz, k - 1], dev(yy, xx + k, zz, cc))
 
-    for dz in (1, 7, 2, 6, 3, 5, 4):
-        send(block(0, 0), block(0, 0), zg_s.at[dz - 1], zg_r.at[dz - 1], dev(yy, xx, zz + dz, cc))
+    def along_z(*steps):
+        for dz in steps:
+            send(block(0, 0), block(0, 0), zg_s.at[dz - 1], zg_r.at[dz - 1], dev(yy, xx, zz + dz, cc))
+
+    along_z(2, 6)
     along_x(0)
+    along_z(1, 7)
     for k, (dx, dc) in enumerate(xc_peers):
         send(labs.at[0], labs.at[dx * NC + dc], la_s.at[k], la_r.at[k], dev(yy, xx + dx, zz, (cc + dc) % NC))
 
@@ -118,18 +122,30 @@
         wn[r, :] = n
         wbf[r, :] = (wf * (1.0 / n)).astype(bf16)
 
+    along_z(3, 5, 4)
+
     def forward(dz):
         landed(block(dz, 0), zg_r.at[dz - 1])
         along_x(dz)
 
+    def neighbours():
+        for k in (1, 3, 2):
+            landed(block(0, k), xa_r.at[0, k - 1])
+            for w, dz in ((0, 1), (1, NZ - 1)):
+                send(block(0, k), block(0, k), xz_s.at[w, k - 1], xz_r.at[w, k - 1], dev(yy, xx, zz + dz, cc))
+
     def share(dz):
+        if dz in (1, NZ - 1):
+            landed(block(dz, 0), zg_r.at[dz - 1])
         for k in (1, 3, 2):
-            landed(block(dz, k), xa_r.at[dz, k - 1])
+            if dz in (1, NZ - 1):
+                landed(block(dz, k), xz_r.at[int(dz != 1), k - 1])
+            elif dz:
+                landed(block(dz, k), xa_r.at[dz, k - 1])
         p = xg.at[(zz + NZ - dz) % NZ, cc]
         send(p, p, sb_s.at[dz], sb_r.at[dz], sib)
 
-    forward(1)
-    forward(7)
+    neighbours()
     share(0)
 
     for k, (dx, dc) in enumerate(xc_peers):
@@ -190,28 +206,22 @@
     forward(2)
     forward(6)
     first_pass(0)
-    share(1)
-    share(7)
     forward(3)
     forward(5)
     forward(4)
+    share(1)
+    share(7)
     first_pass(1)
-    first_pass(7)
     share(2)
     share(6)
+    first_pass(7)
     first_pass(2)
-    first_pass(6)
     share(3)
     share(5)
+    first_pass(6)
     share(4)
     first_pass(3)
     first_pass(5)
-
-    @pl.loop(0, slots)
-    def _(s):
-        c0 = pl.multiple_of(s * 128, 128)
-        wT[:, pl.ds(c0, 128)] = wbf[pl.ds(c0, 128), :].T
-
     first_pass(4)
 
     def reduce_plane(part, first, second, s1, r1, s2, r2):
@@ -237,6 +247,12 @@
         return middle, last
 
     tot_mid, tot_last = reduce_plane(tp, t1, t2, t1_s, t1_r, t2_s, t2_r)
+
+    @pl.loop(0, slots)
+    def _(s):
+        c0 = pl.multiple_of(s * 128, 128)
+        wT[:, pl.ds(c0, 128)] = wbf[pl.ds(c0, 128), :].T
+
     tot_mid()
     total = tot_last()
     inv[...] = scale / total
@@ -442,6 +458,16 @@
     for c in sends:
         c.wait_send()
     for c in stores:
+        c.wait()
+
+
+def store_kernel(*refs):
+    n = len(refs) // 2
+    ins, outs, sem = refs[:n], refs[n:2 * n], refs[2 * n]
+    copies = [pltpu.make_async_copy(a, b, sem.at[k]) for k, (a, b) in enumerate(zip(ins, outs))]
+    for c in copies:
+        c.start()
+    for c in copies:
         c.wait()
 
 
@@ -488,7 +514,7 @@
         vm((NZ, rows, width), bf16),
         vm((NZ - 1, rows, width), bf16),
         dma((2,)), dma((4, 2)),
-        dma((NZ, NX - 1)), dma((NZ, NX - 1)), dma((npeer,)), dma((npeer,)), dma((NZ - 1,)), dma((NZ - 1,)),
+        dma((NZ, NX - 1)), dma((NZ, NX - 1)), dma((2, NX - 1)), dma((2, NX - 1)), dma((npeer,)), dma((npeer,)), dma((NZ - 1,)), dma((NZ - 1,)),
         dma((NZ - 1,)), dma((NZ - 1,)), dma((NZ,)), dma((NZ,)),
         dma((npeer,)), dma((npeer,)), dma((NZ - 1,)), dma((NZ - 1,)),
         dma((npeer,)), dma((npeer,)), dma((NZ - 1,)), dma((NZ - 1,)),
@@ -497,8 +523,9 @@
     ]
     vmem = pl.BlockSpec(memory_space=pltpu.VMEM)
     smem = pl.BlockSpec(memory_space=pltpu.SMEM)
-    hbm = pl.BlockSpec(memory_space=pl.ANY)
-    loss, eg, nw, nv = pl.pallas_call(
+    hbm = pl.BlockSpec(memory_space=pltpu.HBM)
+    place = pl.BlockSpec(memory_space=pl.ANY)
+    results = pl.pallas_call(
         kernel,
         out_shape=(
             jax.ShapeDtypeStruct((1, rows), f32),
@@ -507,10 +534,10 @@
             jax.ShapeDtypeStruct((cols, width), f32),
         ),
         in_specs=[vmem, vmem, smem, smem, hbm, hbm],
-        out_specs=(vmem, vmem, hbm, hbm),
+        out_specs=(vmem, vmem, place, place),
         scratch_shapes=scratch,
         compiler_params=pltpu.CompilerParams(
-            collective_id=0, has_side_effects=True, vmem_limit_bytes=62 * 1024 * 1024
+            collective_id=0, has_side_effects=True, vmem_limit_bytes=44 * 1024 * 1024
         ),
         name="margin_step",
     )(
@@ -518,9 +545,18 @@
         labels.reshape(1, rows),
         block_list,
         counts,
-        centers.reshape(cols, width),
-        momentum.reshape(cols, width),
+        pltpu.with_memory_space_constraint(centers.reshape(cols, width), pltpu.HBM),
+        pltpu.with_memory_space_constraint(momentum.reshape(cols, width), pltpu.HBM),
     )
+    loss, eg, nw, nv = pl.pallas_call(
+        store_kernel,
+        out_shape=tuple(jax.ShapeDtypeStruct(r.shape, r.dtype) for r in results),
+        in_specs=[place] * len(results),
+        out_specs=(hbm,) * len(results),
+        scratch_shapes=[dma((len(results),))],
+        compiler_params=pltpu.CompilerParams(vmem_limit_bytes=1024 * 1024),
+        name="store_results",
+    )(*results)
     return (
         loss.reshape(rows),
         eg,

time: 86.7 us -> 80.2 us (0.925)
  local copies, waits for them, and re-layouts: 7.07 us -> 2.06 us
  Pallas kernels: 77.8 us -> 76.4 us
    unnamed x6, local copies, waits for them, and re-layouts: 7.07 us -> 2.06 us
    pallas_call x1, Pallas kernels: 77.8 us -> 74.2 us  [on_device(): pl.pallas_call(kernel, out_shape=(jax.ShapeDtypeStruct((1, rows), f32), j...]
    pallas_call x0 -> x1, Pallas kernels: none -> 2.25 us  [on_device(): pl.pallas_call(store_kernel, out_shape=tuple((jax.ShapeDtypeStruct(r.shap...]
where the time goes in v3:
time: 80.2 us; the launch traced here: 79.8 us
  Pallas kernels  76.4 us (95%)
  local copies, waits for them, and re-layouts  2.06 us (3%)
  between operations  1.3 us (2%)
    pallas_call x1, Pallas kernels, on_device(): pl.pallas_call(kernel, out_shape=(jax.ShapeDtypeStruct((1, rows), f32), j...  74.2 us
    pallas_call x1, Pallas kernels, on_device(): pl.pallas_call(store_kernel, out_shape=tuple((jax.ShapeDtypeStruct(r.shap...  2.25 us
    unnamed x6, local copies, waits for them, and re-layouts  2.06 us

profile of v3, /device:TPU:1, one launch (start us, length us, event | category | flops | bytes accessed | tf_op | source)
XLA Modules:
  0.0 79.8 jit_solution(6904540662772041824)
XLA Ops:
  1.3 0.0 copy-start
  1.3 0.7 copy-done
  2.0 0.0 copy-start.1
  2.0 0.7 copy-done.1
  2.7 0.0 copy-start.2
  2.7 0.7 copy-done.2
  3.3 74.2 %margin_step.1 = (f32[1,32]{1,0:T(1,128)S(1)}, f32[32,512]{1,0:T(8,128)S(1)}, bf16[1536,512]{1,0:T(8,128)(2,1)S(1)}, f32[1536,512]{1,0:T(8,128)S(1)}) custom-call(bf16[32,512]{1,0:T(8,128)(2,1)S(1)} %copy-done, s32[1,32]{1,0:T(1,128)S(1)} %bitcast.6, s32[12]{0:T(128)S(1)} %copy-done.2, s32[1]{0:T(128)S(6)} %copy.10.cnt_ref, bf16[1536,512]{1,0:T(8,128)(2,1)} %bitcast.8, ...), custom_call_target="tpu_custom_call" | custom-call | tf_op jit(solution)/shard_map/margin_step/pallas_call | solution.py:528
  77.5 2.2 %store_results.1 = (f32[1,32]{1,0:T(1,128)}, f32[32,512]{1,0:T(8,128)}, bf16[1536,512]{1,0:T(8,128)(2,1)}, f32[1536,512]{1,0:T(8,128)}) custom-call(f32[1,32]{1,0:T(1,128)S(1)} %get-tuple-element.12.refs_0_, f32[32,512]{1,0:T(8,128)S(1)} %get-tuple-element.13.refs_1_, bf16[1536,512]{1,0:T(8,128)(2,1)S(1)} %get-tuple-element.14.refs_2_, ...), custom_call_target="tpu_custom_call" | custom-call | tf_op jit(solution)/shard_map/store_results/pallas_call | solution.py:551
Async XLA Ops:
  1.3 0.8 copy-start
  2.0 0.7 copy-start.1
  2.7 0.7 copy-start.2

commit v4 on v3

--- a/solution.py
+++ b/solution.py
@@ -29,9 +29,9 @@
 
 
 def kernel(
-    emb_ref, lab_ref, ids_ref, cnt_ref, cen_hbm, mom_hbm,
+    emb_hbm, lab_hbm, ids_hbm, cnt_ref, cen_hbm, mom_hbm,
     loss_ref, eg_ref, nw_hbm, nv_hbm,
-    cen, mom, wbf, wT, wn, xg, labs, labz, tgt, ez, err, tp, pp, t1, t2, p1, p2, inv,
+    emb_ref, lab_ref, ids_ref, cen, mom, wbf, wT, wn, xg, labs, labz, tgt, ez, err, tp, pp, t1, t2, p1, p2, inv,
     pt, pf, gs, r2, rP, rM,
     gown, goth, pr, xs, xr, zs, zr,
     ldsem, stsem,
@@ -76,6 +76,14 @@
 
     ld_cen = pltpu.make_async_copy(cen_hbm, cen, ldsem.at[0])
     ld_mom = pltpu.make_async_copy(mom_hbm, mom, ldsem.at[1])
+    small = [
+        pltpu.make_async_copy(a, b, ldsem.at[2 + k])
+        for k, (a, b) in enumerate(
+            ((emb_hbm, emb_ref), (lab_hbm, lab_ref), (ids_hbm, ids_ref))
+        )
+    ]
+    for c in small:
+        c.start()
     ld_cen.start()
     ld_mom.start()
     barrier = pltpu.get_barrier_semaphore()
@@ -85,6 +93,8 @@
     for d in greet:
         pl.semaphore_signal(barrier, inc=1, device_id=d, device_id_type=MESH)
 
+    for c in small:
+        c.wait()
     xf = emb_ref[...].astype(f32)
     xn = jnp.sqrt(jnp.sum(xf * xf, axis=1, keepdims=True) + tiny_eps)
     xu = xf / xn
@@ -377,10 +387,10 @@
 
     pos_mid, pos_last = reduce_plane(pp, p1, p2, p1_s, p1_r, p2_s, p2_r)
     merge(0)
+    row_grad(0, group2)
+    pair(0)
     to_y(pt.at[1, 3], rP.at[3], 10, yup)
     to_y(pt.at[2, 1], rM.at[1], 11, ydn)
-    row_grad(0, group2)
-    pair(0)
     merge(1)
     pf[2] = center_grad(yy)
     rows_x(0)
@@ -425,13 +435,19 @@
     update(yy, 0, 4, 0)
     onward(0)
     rows_z(0)
+    landed(gs.at[qm, 2], yg_r.at[0, 2])
+    landed(gs.at[qp, 0], yg_r.at[1, 0])
+    for n, (q, p) in enumerate(((qm, 0), (qm, 2), (qp, 0), (qp, 2))):
+        update(q, p, 1, 1 + n)
     onward(1)
+    landed(gs.at[qm, 3], yg_r.at[0, 3])
+    landed(gs.at[qp, 1], yg_r.at[1, 1])
+    for n, (q, p) in enumerate(((qm, 1), (qm, 3), (qp, 1), (qp, 3))):
+        update(q, p, 1, 5 + n)
     rows_z(1)
-    for n in range(2):
-        landed(gs.at[qm, 2 + n], yg_r.at[0, 2 + n])
-        landed(gs.at[qp, n], yg_r.at[1, n])
-    update(qm, 0, 4, 1)
-    update(qp, 0, 4, 2)
+    for n, p in enumerate((0, 2)):
+        landed(gs.at[q2, p], yg_r.at[2, p])
+        update(q2, p, 1, 9 + n)
 
     gx = gown[NZ // 2, pl.ds(xrow, rows), :]
     for dz in range(1, NZ):
@@ -450,10 +466,9 @@
             mine = jnp.where(here, line[:, at:at + rows], mine)
     loss_ref[...] = mine
 
-    for n in range(2):
-        landed(gs.at[q2, n], yg_r.at[2, n])
-        landed(gs.at[q2, 2 + n], yg_r.at[2, 2 + n])
-    update(q2, 0, 4, 3)
+    for n, p in enumerate((1, 3)):
+        landed(gs.at[q2, p], yg_r.at[2, p])
+        update(q2, p, 1, 11 + n)
 
     for c in sends:
         c.wait_send()
@@ -469,6 +484,10 @@
         c.start()
     for c in copies:
         c.wait()
+
+
+def in_hbm(a):
+    return pltpu.with_memory_space_constraint(a, pltpu.HBM)
 
 
 def on_device(embeddings, labels, centers, momentum, block_list, counts):
@@ -482,6 +501,9 @@
     vm, dma = pltpu.VMEM, pltpu.SemaphoreType.DMA
     npeer = NX * NC - 1
     scratch = [
+        vm((rows, width), bf16),
+        vm((1, rows), i32),
+        pltpu.SMEM((slots,), i32),
         vm((cols, width), bf16),
         vm((cols, width), f32),
         vm((cols, width), bf16),
@@ -513,7 +535,7 @@
         vm((2, NX - 1, NZ // 2, rows, width), bf16),
         vm((NZ, rows, width), bf16),
         vm((NZ - 1, rows, width), bf16),
-        dma((2,)), dma((4, 2)),
+        dma((5,)), dma((13, 2)),
         dma((NZ, NX - 1)), dma((NZ, NX - 1)), dma((2, NX - 1)), dma((2, NX - 1)), dma((npeer,)), dma((npeer,)), dma((NZ - 1,)), dma((NZ - 1,)),
         dma((NZ - 1,)), dma((NZ - 1,)), dma((NZ,)), dma((NZ,)),
         dma((npeer,)), dma((npeer,)), dma((NZ - 1,)), dma((NZ - 1,)),
@@ -522,7 +544,6 @@
         dma((2, NX - 1)), dma((2, NX - 1)), dma((NZ - 1,)), dma((NZ - 1,)),
     ]
     vmem = pl.BlockSpec(memory_space=pltpu.VMEM)
-    smem = pl.BlockSpec(memory_space=pltpu.SMEM)
     hbm = pl.BlockSpec(memory_space=pltpu.HBM)
     place = pl.BlockSpec(memory_space=pl.ANY)
     results = pl.pallas_call(
@@ -533,7 +554,7 @@
             jax.ShapeDtypeStruct((cols, width), bf16),
             jax.ShapeDtypeStruct((cols, width), f32),
         ),
-        in_specs=[vmem, vmem, smem, smem, hbm, hbm],
+        in_specs=[hbm, hbm, hbm, pl.BlockSpec(memory_space=pltpu.SMEM), hbm, hbm],
         out_specs=(vmem, vmem, place, place),
         scratch_shapes=scratch,
         compiler_params=pltpu.CompilerParams(
@@ -541,12 +562,12 @@
         ),
         name="margin_step",
     )(
-        embeddings,
-        labels.reshape(1, rows),
-        block_list,
+        in_hbm(embeddings),
+        in_hbm(labels.reshape(1, rows)),
+        in_hbm(block_list),
         counts,
-        pltpu.with_memory_space_constraint(centers.reshape(cols, width), pltpu.HBM),
-        pltpu.with_memory_space_constraint(momentum.reshape(cols, width), pltpu.HBM),
+        in_hbm(centers.reshape(cols, width)),
+        in_hbm(momentum.reshape(cols, width)),
     )
     loss, eg, nw, nv = pl.pallas_call(
         store_kernel,

time: 80.2 us -> 80 us (level)
  local copies, waits for them, and re-layouts: 2.06 us -> 0 us
  Pallas kernels: 76.4 us -> 77.8 us
    unnamed x6 -> x0, local copies, waits for them, and re-layouts: 2.06 us -> none
    pallas_call x1, Pallas kernels: 74.2 us -> 75.5 us  [on_device(): pl.pallas_call(kernel, out_shape=(jax.ShapeDtypeStruct((1, rows), f32), j...]
where the time goes in v4:
time: 80 us; the launch traced here: 79.1 us
  Pallas kernels  77.8 us (97%)
  between operations  1.29 us (2%)
    pallas_call x1, Pallas kernels, on_device(): pl.pallas_call(kernel, out_shape=(jax.ShapeDtypeStruct((1, rows), f32), j...  75.5 us
    pallas_call x1, Pallas kernels, on_device(): pl.pallas_call(store_kernel, out_shape=tuple((jax.ShapeDtypeStruct(r.shap...  2.25 us

profile of v4, /device:TPU:1, one launch (start us, length us, event | category | flops | bytes accessed | tf_op | source)
XLA Modules:
  0.0 79.1 jit_solution(18005335593623690199)
XLA Ops:
  1.3 75.5 %margin_step.1 = (f32[1,32]{1,0:T(1,128)S(1)}, f32[32,512]{1,0:T(8,128)S(1)}, bf16[1536,512]{1,0:T(8,128)(2,1)S(1)}, f32[1536,512]{1,0:T(8,128)S(1)}) custom-call(bf16[32,512]{1,0:T(8,128)(2,1)} %emb_hbm.1, s32[1,32]{1,0:T(1,128)} %bitcast.8, s32[12]{0:T(128)} %ids_hbm.1, s32[1]{0:T(128)S(6)} %copy.10.cnt_ref, bf16[1536,512]{1,0:T(8,128)(2,1)} %bitcast.7, ...), custom_call_target="tpu_custom_call" | custom-call | tf_op jit(solution)/shard_map/margin_step/pallas_call | solution.py:549
  76.8 2.2 %store_results.1 = (f32[1,32]{1,0:T(1,128)}, f32[32,512]{1,0:T(8,128)}, bf16[1536,512]{1,0:T(8,128)(2,1)}, f32[1536,512]{1,0:T(8,128)}) custom-call(f32[1,32]{1,0:T(1,128)S(1)} %get-tuple-element.12.refs_0_, f32[32,512]{1,0:T(8,128)S(1)} %get-tuple-element.13.refs_1_, bf16[1536,512]{1,0:T(8,128)(2,1)S(1)} %get-tuple-element.14.refs_2_, ...), custom_call_target="tpu_custom_call" | custom-call | tf_op jit(solution)/shard_map/store_results/pallas_call | solution.py:572

commit v5 on v4

--- a/solution.py
+++ b/solution.py
@@ -234,15 +234,15 @@
     first_pass(5)
     first_pass(4)
 
-    def reduce_plane(part, first, second, s1, r1, s2, r2):
+    def reduce_plane(part, near, second, s1, r1, s2, r2):
         for k, (dx, dc) in enumerate(xc_peers):
-            send(part, first.at[k], s1.at[k], r1.at[k], dev(yy, xx + dx, zz, (cc + dc) % NC))
+            send(part, near.at[k], s1.at[k], r1.at[k], dev(yy, xx + dx, zz, (cc + dc) % NC))
 
         def middle():
             acc = part[...]
             for k in range(len(xc_peers)):
-                landed(first.at[k], r1.at[k])
-                acc = acc + first[k]
+                landed(near.at[k], r1.at[k])
+                acc = acc + near[k]
             second[0] = acc
             for dz in range(1, NZ):
                 send(second.at[0], second.at[dz], s2.at[dz - 1], r2.at[dz - 1], dev(yy, xx, zz + dz, cc))
@@ -339,12 +339,13 @@
         landed(gs.at[qp, 2 + n], yg_r.at[1, 2 + n])
         send(gs.at[qp, 2 + n], gs.at[qp, 2 + n], yg_s.at[2, 2 + n], yg_r.at[2, 2 + n], ydn)
 
-    group2 = NZ // 2
+    group2 = 2
+    first = 2
 
     def row_grad(lo, hi):
         @pl.loop(lo, hi)
         def _(i):
-            z = (zz + NZ // 2 + i) % NZ
+            z = (zz + first + i) % NZ
             lanes = pl.ds(pl.multiple_of(z * zrows, zrows), zrows)
             gx = nn_dot(wT[...], err[:, lanes]).T
             a, b = gx[: zrows // 2], gx[zrows // 2:]
@@ -375,7 +376,7 @@
             landed(xr.at[g, k - 1], xs_r.at[g, k - 1])
         for n in range(group2):
             i = g * group2 + n
-            dz = (NZ // 2 + i) % NZ
+            dz = (first + i) % NZ
             h = gown[i, pl.ds(xrow, rows), :]
             for k in range(1, NX):
                 h = h + xr[g, k - 1, n].astype(f32)
@@ -386,21 +387,27 @@
                 send(zs.at[i], zr.at[dz - 1], zs_s.at[dz - 1], zs_r.at[dz - 1], dev(yy, xx, zz + dz, cc))
 
     pos_mid, pos_last = reduce_plane(pp, p1, p2, p1_s, p1_r, p2_s, p2_r)
+    row_grad(0, 2)
+    pair(0)
     merge(0)
-    row_grad(0, group2)
-    pair(0)
+    row_grad(2, 4)
+    pair(1)
+    rows_x(0)
     to_y(pt.at[1, 3], rP.at[3], 10, yup)
     to_y(pt.at[2, 1], rM.at[1], 11, ydn)
     merge(1)
+    row_grad(4, 6)
+    pair(2)
+    rows_x(1)
     pf[2] = center_grad(yy)
-    rows_x(0)
-    row_grad(group2, group2 + 2)
     own(0)
-    row_grad(group2 + 2, NZ)
-    pair(1)
+    row_grad(6, 8)
+    pair(3)
+    rows_x(2)
     pos_mid()
+    rows_x(3)
     own(1)
-    rows_x(1)
+    rows_z(0)
 
     ld_mom.wait()
     tile = 32
@@ -433,23 +440,26 @@
             stores.append(c)
 
     update(yy, 0, 4, 0)
+    rows_z(1)
     onward(0)
-    rows_z(0)
     landed(gs.at[qm, 2], yg_r.at[0, 2])
     landed(gs.at[qp, 0], yg_r.at[1, 0])
-    for n, (q, p) in enumerate(((qm, 0), (qm, 2), (qp, 0), (qp, 2))):
+    for n, (q, p) in enumerate(((qm, 0), (qm, 2))):
         update(q, p, 1, 1 + n)
+    rows_z(2)
+    for n, (q, p) in enumerate(((qp, 0), (qp, 2))):
+        update(q, p, 1, 3 + n)
+    rows_z(3)
     onward(1)
     landed(gs.at[qm, 3], yg_r.at[0, 3])
     landed(gs.at[qp, 1], yg_r.at[1, 1])
     for n, (q, p) in enumerate(((qm, 1), (qm, 3), (qp, 1), (qp, 3))):
         update(q, p, 1, 5 + n)
-    rows_z(1)
     for n, p in enumerate((0, 2)):
         landed(gs.at[q2, p], yg_r.at[2, p])
         update(q2, p, 1, 9 + n)
 
-    gx = gown[NZ // 2, pl.ds(xrow, rows), :]
+    gx = gown[NZ - first, pl.ds(xrow, rows), :]
     for dz in range(1, NZ):
         landed(zr.at[dz - 1], zs_r.at[dz - 1])
         gx = gx + zr[dz - 1].astype(f32)
@@ -531,8 +541,8 @@
         vm((NZ, NX * rows, width), f32),
         vm((NZ, NX * rows, width), bf16),
         vm((NZ, NX * rows, width), bf16),
-        vm((2, NX, NZ // 2, rows, width), bf16),
-        vm((2, NX - 1, NZ // 2, rows, width), bf16),
+        vm((4, NX, NZ // 4, rows, width), bf16),
+        vm((4, NX - 1, NZ // 4, rows, width), bf16),
         vm((NZ, rows, width), bf16),
         vm((NZ - 1, rows, width), bf16),
         dma((5,)), dma((13, 2)),
@@ -540,8 +550,8 @@
         dma((NZ - 1,)), dma((NZ - 1,)), dma((NZ,)), dma((NZ,)),
         dma((npeer,)), dma((npeer,)), dma((NZ - 1,)), dma((NZ - 1,)),
         dma((npeer,)), dma((npeer,)), dma((NZ - 1,)), dma((NZ - 1,)),
-        dma((12,)), dma((12,)), dma((3, 4)), dma((3, 4)), dma((2,)), dma((2,)),
-        dma((2, NX - 1)), dma((2, NX - 1)), dma((NZ - 1,)), dma((NZ - 1,)),
+        dma((12,)), dma((12,)), dma((3, 4)), dma((3, 4)), dma((4,)), dma((4,)),
+        dma((4, NX - 1)), dma((4, NX - 1)), dma((NZ - 1,)), dma((NZ - 1,)),
     ]
     vmem = pl.BlockSpec(memory_space=pltpu.VMEM)
     hbm = pl.BlockSpec(memory_space=pltpu.HBM)

time: 80 us -> 77.4 us (0.968); the launches traced: 79.1 us -> 77.3 us
  Pallas kernels: 77.8 us -> 76.1 us
    pallas_call x1, Pallas kernels: 75.5 us -> 73.8 us  [on_device(): pl.pallas_call(kernel, out_shape=(jax.ShapeDtypeStruct((1, rows), f32), j...]
where the time goes in v5:
time: 77.4 us; the launch traced here: 77.3 us
  Pallas kernels  76.1 us (98%)
  between operations  1.29 us (2%)
    pallas_call x1, Pallas kernels, on_device(): pl.pallas_call(kernel, out_shape=(jax.ShapeDtypeStruct((1, rows), f32), j...  73.8 us
    pallas_call x1, Pallas kernels, on_device(): pl.pallas_call(store_kernel, out_shape=tuple((jax.ShapeDtypeStruct(r.shap...  2.25 us

profile of v5, /device:TPU:1, one launch (start us, length us, event | category | flops | bytes accessed | tf_op | source)
XLA Modules:
  0.0 77.3 jit_solution(4510445614494693628)
XLA Ops:
  1.3 73.8 %margin_step.1 = (f32[1,32]{1,0:T(1,128)S(1)}, f32[32,512]{1,0:T(8,128)S(1)}, bf16[1536,512]{1,0:T(8,128)(2,1)S(1)}, f32[1536,512]{1,0:T(8,128)S(1)}) custom-call(bf16[32,512]{1,0:T(8,128)(2,1)} %emb_hbm.1, s32[1,32]{1,0:T(1,128)} %bitcast.8, s32[12]{0:T(128)} %ids_hbm.1, s32[1]{0:T(128)S(6)} %copy.10.cnt_ref, bf16[1536,512]{1,0:T(8,128)(2,1)} %bitcast.7, ...), custom_call_target="tpu_custom_call" | custom-call | tf_op jit(solution)/shard_map/margin_step/pallas_call | solution.py:559
  75.1 2.2 %store_results.1 = (f32[1,32]{1,0:T(1,128)}, f32[32,512]{1,0:T(8,128)}, bf16[1536,512]{1,0:T(8,128)(2,1)}, f32[1536,512]{1,0:T(8,128)}) custom-call(f32[1,32]{1,0:T(1,128)S(1)} %get-tuple-element.12.refs_0_, f32[32,512]{1,0:T(8,128)S(1)} %get-tuple-element.13.refs_1_, bf16[1536,512]{1,0:T(8,128)(2,1)S(1)} %get-tuple-element.14.refs_2_, ...), custom_call_target="tpu_custom_call" | custom-call | tf_op jit(solution)/shard_map/store_results/pallas_call | solution.py:582

commit v6 on v5

--- a/solution.py
+++ b/solution.py
@@ -327,11 +327,15 @@
             landed(rM.at[p], ys_r.at[(8 + n) if p >= 2 else (5 if n == 0 else 11)])
             s = pf[2, pl.ds(p * piece, piece), :] + rP[p].astype(f32) + rM[p].astype(f32)
             gs[yy, p] = s.astype(bf16)
-        for p, q in ((n, 2 + n),):
-            send(gs.at[yy, p], gs.at[yy, p], yg_s.at[0, p], yg_r.at[0, p], yup)
-            send(gs.at[yy, q], gs.at[yy, q], yg_s.at[1, q], yg_r.at[1, q], ydn)
-            send(gs.at[yy, q], gs.at[yy, q], yg_s.at[0, q], yg_r.at[0, q], yup)
-            send(gs.at[yy, p], gs.at[yy, p], yg_s.at[1, p], yg_r.at[1, p], ydn)
+        spread(0, n, yup)
+        spread(1, 2 + n, ydn)
+
+    def spread(way, p, to):
+        send(gs.at[yy, p], gs.at[yy, p], yg_s.at[way, p], yg_r.at[way, p], to)
+
+    def rest(n):
+        spread(0, 2 + n, yup)
+        spread(1, n, ydn)
 
     def onward(n):
         landed(gs.at[qm, n], yg_r.at[0, n])
@@ -407,6 +411,7 @@
     pos_mid()
     rows_x(3)
     own(1)
+    rest(0)
     rows_z(0)
 
     ld_mom.wait()
@@ -440,24 +445,23 @@
             stores.append(c)
 
     update(yy, 0, 4, 0)
+    onward(0)
+    rest(1)
     rows_z(1)
-    onward(0)
-    landed(gs.at[qm, 2], yg_r.at[0, 2])
-    landed(gs.at[qp, 0], yg_r.at[1, 0])
-    for n, (q, p) in enumerate(((qm, 0), (qm, 2))):
+    for n, (q, p) in enumerate(((qm, 0), (qp, 2))):
         update(q, p, 1, 1 + n)
     rows_z(2)
-    for n, (q, p) in enumerate(((qp, 0), (qp, 2))):
+    onward(1)
+    rows_z(3)
+    for n, (q, p) in enumerate(((qm, 1), (qp, 3))):
         update(q, p, 1, 3 + n)
-    rows_z(3)
-    onward(1)
-    landed(gs.at[qm, 3], yg_r.at[0, 3])
-    landed(gs.at[qp, 1], yg_r.at[1, 1])
-    for n, (q, p) in enumerate(((qm, 1), (qm, 3), (qp, 1), (qp, 3))):
-        update(q, p, 1, 5 + n)
+    landed(gs.at[qm, 2], yg_r.at[0, 2])
+    update(qm, 2, 1, 5)
+    landed(gs.at[qp, 0], yg_r.at[1, 0])
+    update(qp, 0, 1, 6)
     for n, p in enumerate((0, 2)):
         landed(gs.at[q2, p], yg_r.at[2, p])
-        update(q2, p, 1, 9 + n)
+        update(q2, p, 1, 7 + n)
 
     gx = gown[NZ - first, pl.ds(xrow, rows), :]
     for dz in range(1, NZ):
@@ -476,6 +480,10 @@
             mine = jnp.where(here, line[:, at:at + rows], mine)
     loss_ref[...] = mine
 
+    landed(gs.at[qm, 3], yg_r.at[0, 3])
+    update(qm, 3, 1, 9)
+    landed(gs.at[qp, 1], yg_r.at[1, 1])
+    update(qp, 1, 1, 10)
     for n, p in enumerate((1, 3)):
         landed(gs.at[q2, p], yg_r.at[2, p])
         update(q2, p, 1, 11 + n)

time: 77.4 us -> 75.5 us (0.975)
  Pallas kernels: 76.1 us -> 74.1 us
    pallas_call x1, Pallas kernels: 73.8 us -> 71.8 us  [on_device(): pl.pallas_call(kernel, out_shape=(jax.ShapeDtypeStruct((1, rows), f32), j...]
where the time goes in v6:
time: 75.5 us; the launch traced here: 75.4 us
  Pallas kernels  74.1 us (98%)
  between operations  1.29 us (2%)
    pallas_call x1, Pallas kernels, on_device(): pl.pallas_call(kernel, out_shape=(jax.ShapeDtypeStruct((1, rows), f32), j...  71.8 us
    pallas_call x1, Pallas kernels, on_device(): pl.pallas_call(store_kernel, out_shape=tuple((jax.ShapeDtypeStruct(r.shap...  2.25 us

profile of v6, /device:TPU:1, one launch (start us, length us, event | category | flops | bytes accessed | tf_op | source)
XLA Modules:
  0.0 75.4 jit_solution(17880308534905389148)
XLA Ops:
  1.3 71.8 %margin_step.1 = (f32[1,32]{1,0:T(1,128)S(1)}, f32[32,512]{1,0:T(8,128)S(1)}, bf16[1536,512]{1,0:T(8,128)(2,1)S(1)}, f32[1536,512]{1,0:T(8,128)S(1)}) custom-call(bf16[32,512]{1,0:T(8,128)(2,1)} %emb_hbm.1, s32[1,32]{1,0:T(1,128)} %bitcast.8, s32[12]{0:T(128)} %ids_hbm.1, s32[1]{0:T(128)S(6)} %copy.10.cnt_ref, bf16[1536,512]{1,0:T(8,128)(2,1)} %bitcast.7, ...), custom_call_target="tpu_custom_call" | custom-call | tf_op jit(solution)/shard_map/margin_step/pallas_call | solution.py:567
  73.1 2.2 %store_results.1 = (f32[1,32]{1,0:T(1,128)}, f32[32,512]{1,0:T(8,128)}, bf16[1536,512]{1,0:T(8,128)(2,1)}, f32[1536,512]{1,0:T(8,128)}) custom-call(f32[1,32]{1,0:T(1,128)S(1)} %get-tuple-element.12.refs_0_, f32[32,512]{1,0:T(8,128)S(1)} %get-tuple-element.13.refs_1_, bf16[1536,512]{1,0:T(8,128)(2,1)S(1)} %get-tuple-element.14.refs_2_, ...), custom_call_target="tpu_custom_call" | custom-call | tf_op jit(solution)/shard_map/store_results/pallas_call | solution.py:590
